TPU v7x, 128 devices: a whole 4x4x4 slice. The times are simulated.
128 devices in a mesh: dom: 16 (over x_hi, z, core), slab: 8 (over y, x_lo).
Axes of the slice: x: 4 (x_hi: 2, x_lo: 2; x = x_hi * 2 + x_lo), y: 4, z: 4, core: 2. Of those that a mesh axis runs over, the one named last changes fastest.
Arguments:
- displacement: float32 [3, 5, 5, 5, 32, 2048], P(None, None, None, None, 'dom', 'slab'), may hold values from -0.6 to 0.6
- velocity: float32 [3, 5, 5, 5, 32, 2048], P(None, None, None, None, 'dom', 'slab'), may hold values from -6 to 6
- lame_lambda: float32 [5, 5, 5, 32, 2048], P(None, None, None, 'dom', 'slab'), may hold values from 0.5 to 1.5
- shear_modulus: float32 [5, 5, 5, 32, 2048], P(None, None, None, 'dom', 'slab'), may hold values from 0.3 to 1.2
- density: float32 [5, 5, 5, 32, 2048], P(None, None, None, 'dom', 'slab'), may hold values from 0.7 to 1.4
- traces: bfloat16 [32768, 3072], P(('dom', 'slab')), may hold values from -6 to 6
- section_weights: bfloat16 [4, 256], replicated, may hold values from -0.375 to 0.375
- owner: int32 [32768, 1], P(('dom', 'slab')), may hold values from 0 to 127; in each aligned block of 256 rows (0 to 255, 256 to 511, ...) at most 4 rows name the same one
- element_idx: int32 [32768], P(('dom', 'slab')), may hold values from 0 to 511
- node_weights: bfloat16 [32768, 125], P(('dom', 'slab')), may hold values from -1.796875 to 1.796875
- encode_bits: int32 [32768, 4], P(('dom', 'slab')), may hold values from 0 to 1
Outputs:
- disp_out: float32 [3, 5, 5, 5, 32, 2048], P(None, None, None, None, 'dom', 'slab')
- veloc_out: float32 [3, 5, 5, 5, 32, 2048], P(None, None, None, None, 'dom', 'slab')
Inputs may be any that keep to these rules, and one draw needn't show every extreme that they name: Among the rows of one device at most 4 name the same owner, a bound that some of them reach.
All inputs are finite; a program needn't handle non-finite values.
Results may differ from a plain program's by a relative error of at most 0.0006.
Values may be sent and summed in bfloat16 or wider, within the bound.
A program may use at most 128 MiB of HBM per device.

v0:
```python
import functools
import math

import jax
import jax.numpy as jnp
import numpy as np
from jax import lax
from jax.experimental import pallas as pl
from jax.experimental.pallas import tpu as pltpu
from jax.sharding import PartitionSpec as P

EC = 128
CAP = 4
G = 4
STEPS = 4
DT = 0.025
NODES6 = 150
HI, LO, EL = 160, 176, 192
F32, BF16 = jnp.float32, jnp.bfloat16
MESH = pl.DeviceIdType.MESH


def gll():
    inner_point = math.sqrt(3.0 / 7.0)
    points = np.array([-1.0, -inner_point, 0.0, inner_point, 1.0])
    weights = np.array([0.1, 49.0 / 90.0, 32.0 / 45.0, 49.0 / 90.0, 0.1])
    legendre = (35.0 * points**4 - 30.0 * points**2 + 3.0) / 8.0
    derivative = np.zeros((5, 5))
    for i in range(5):
        for j in range(5):
            if i != j:
                derivative[i, j] = legendre[i] / (legendre[j] * (points[i] - points[j]))
    derivative[0, 0] = -5.0
    derivative[4, 4] = 5.0
    return 2.0 * derivative, weights


D2, WEIGHTS = gll()
FORWARD, BACKWARD = D2, -D2.T


def pack_kernel(devices, traces, weights, owner, element, nodew, bits, out, wsel):
    rows = traces.shape[0]
    nt = weights.shape[1]
    signs = (2 * bits[...] - 1).astype(F32).T.astype(BF16)
    wsel[...] = jnp.zeros_like(wsel)
    for c in range(3):
        wsel[c, c * STEPS : (c + 1) * STEPS, :] = weights[...].astype(F32)
    source = jnp.zeros((rows, 128), F32)
    for g in range(G):
        sign = signs[:, g : g + 1]
        for c in range(3):
            first = (g * 3 + c) * nt
            block = traces[:, first : first + nt] * sign
            source = source + lax.dot_general(
                block,
                wsel[c].astype(BF16),
                (((1,), (1,)), ((), ())),
                preferred_element_type=F32,
            )
    high = source.astype(BF16).astype(F32)
    low = source - high
    lane = lax.broadcasted_iota(jnp.int32, (rows, 128), 1)
    where_el = jnp.broadcast_to(element[...], (128, rows)).astype(F32).T
    el_high = jnp.floor(where_el * (1.0 / 256.0))
    el_low = where_el - 256.0 * el_high
    base = HI - 128
    extra = pltpu.roll(high, base, 1) + pltpu.roll(low, LO - 128, 1)
    extra = jnp.where(lane == EL - 128, el_low, extra)
    extra = jnp.where(lane == EL - 127, el_high, extra)
    node = lax.broadcasted_iota(jnp.int32, (125, 256), 0)
    column = lax.broadcasted_iota(jnp.int32, (125, 256), 1)
    slot6 = (node // 5) * 6 + node % 5
    spread = (column == slot6) | ((node % 5 == 4) & (column == slot6 + 1))
    wide = jnp.dot(nodew[...], spread.astype(F32).astype(BF16), preferred_element_type=F32)
    right = jnp.concatenate([wide[:, :128], wide[:, 128:] + extra], axis=1).astype(BF16)
    device = lax.broadcasted_iota(jnp.int32, (devices, rows), 0)
    member = (owner[...] == device).astype(F32)
    earlier = lax.broadcasted_iota(jnp.int32, (rows, rows), 0) < lax.broadcasted_iota(
        jnp.int32, (rows, rows), 1
    )
    before = jnp.dot(
        member.astype(BF16), earlier.astype(F32).astype(BF16), preferred_element_type=F32
    )
    for k in range(CAP):
        choose = jnp.where(before == float(k), member, 0.0).astype(BF16)
        packed = jnp.dot(choose, right, preferred_element_type=F32)
        out[:, k * 256 : (k + 1) * 256] = packed.astype(BF16)


def line(m, u):
    e0, e1, o0, o1 = u[0] + u[4], u[1] + u[3], u[0] - u[4], u[1] - u[3]
    even, odd = [], []
    for i in range(2):
        ce = [float((m[i, l] + m[i, 4 - l]) / 2) for l in range(2)]
        co = [float((m[i, l] - m[i, 4 - l]) / 2) for l in range(2)]
        even.append(ce[0] * e0 + ce[1] * e1 + float(m[i, 2]) * u[2])
        odd.append(co[0] * o0 + co[1] * o1)
    middle = float(m[2, 0]) * o0 + float(m[2, 1]) * o1
    return [even[0] + odd[0], even[1] + odd[1], middle, odd[1] - even[1], odd[0] - even[0]]


def half_row(lower, upper, half):
    return jnp.where(half == 0, float(lower), float(upper)).astype(F32)


def kline(m, p0, p1, p2, half):
    first = half == 0
    ce = [[(m[i, l] + m[i, 4 - l]) / 2 for l in range(2)] for i in range(2)]
    co = [[(m[i, l] - m[i, 4 - l]) / 2 for l in range(2)] for i in range(2)]
    back = jnp.where(first, p2, p1)
    even, odd = p0 + back, p0 - back
    mid = jnp.where(first, p1, pltpu.roll(p1, 4, 1))
    evens, odds = pltpu.roll(even, 4, 1), pltpu.roll(odd, 4, 1)
    eout = (
        half_row(ce[0][0], ce[1][1], half) * even
        + half_row(ce[0][1], ce[1][0], half) * evens
        + half_row(m[0, 2], m[1, 2], half) * mid
    )
    oout = half_row(co[0][0], co[1][1], half) * odd + half_row(co[0][1], co[1][0], half) * odds
    q0 = eout + oout
    q43 = oout - eout
    q22 = half_row(m[2, 0], m[2, 1], half) * odd + half_row(m[2, 1], m[2, 0], half) * odds
    q1 = jnp.where(first, q22, q43)
    q2 = jnp.where(first, q43, pltpu.roll(q43, 4, 1))
    return q0, q1, q2


SIDES = [(-1, 0), (1, 0), (0, -1), (0, 1), (-1, -1), (-1, 1), (1, -1), (1, 1)]
OPPOSITE = [1, 0, 3, 2, 7, 6, 5, 4]


def message_rows(side, comps):
    if side < 4:
        return comps * 8
    return comps + (comps + 1) // 2


def step_kernel(
    nd,
    ns,
    disp,
    veloc,
    lame,
    shear,
    density,
    got,
    disp_out,
    veloc_out,
    U,
    W,
    LAM,
    MU,
    CM,
    GR,
    SG,
    F,
    DEP,
    TT,
    OH,
    *rest,
):
    send, recv = rest[0:8], rest[8:16]
    send_sem, recv_sem = rest[16], rest[17]
    dom, slab = lax.axis_index("dom"), lax.axis_index("slab")

    def exists(side):
        da, db = SIDES[side]
        cond = None
        for shift, index, count in ((da, dom, nd), (db, slab, ns)):
            if shift:
                one = index > 0 if shift < 0 else index < count - 1
                cond = one if cond is None else jnp.logical_and(cond, one)
        return cond

    def target(side):
        return (dom + SIDES[side][0], slab + SIDES[side][1])

    for side in range(8):
        recv[side][...] = jnp.zeros_like(recv[side])
    barrier = pltpu.get_barrier_semaphore()
    count = 0
    for side in range(8):
        count = count + exists(side).astype(jnp.int32)

        @pl.when(exists(side))
        def _():
            pl.semaphore_signal(barrier, inc=1, device_id=target(side), device_id_type=MESH)

    sub = lax.broadcasted_iota(jnp.int32, (1, 8, 128), 1)
    lane = lax.broadcasted_iota(jnp.int32, (1, 8, 128), 2)
    half, bit_b, bit_a = sub // 4, (sub // 2) % 2, sub % 2

    def roll_s(x, shift):
        return pltpu.roll(x, shift % 8, 1)

    def roll_l(x, shift):
        return pltpu.roll(x, shift % 128, 2)

    def load_pairs(dst, src):
        lead = (slice(None),) * (len(dst.shape) - 3)
        for kp in range(3):
            dst[lead + (kp, slice(0, 4))] = src[lead + (2 * kp,)]
            dst[lead + (kp, slice(4, 8))] = src[lead + (min(2 * kp + 1, 4),)]

    def store_pairs(dst, src):
        lead = (slice(None),) * (len(src.shape) - 3)
        for k in range(5):
            first = 4 * (k % 2)
            dst[lead + (k,)] = src[lead + (k // 2, slice(first, first + 4))]

    def local_sums(comps):
        for c in range(comps):
            for i in range(5):
                p0, p2 = F[c, i, :, 0], F[c, i, :, 2]
                dup = jnp.where(half == 0, p0, roll_s(p0, 4))
                F[c, i, :, 0] = p0 + jnp.where((half == 0) & (lane > 0), roll_l(p2, 1), 0.0)
                F[c, i, :, 2] = p2 + jnp.where(lane < 127, roll_l(dup, -1), 0.0)
            for j in range(5):
                x0, x4 = F[c, 0, j], F[c, 4, j]
                F[c, 0, j] = x0 + jnp.where(bit_a == 1, roll_s(x4, 1), 0.0)
                F[c, 4, j] = x4 + jnp.where(bit_a == 0, roll_s(x0, -1), 0.0)
            for i in range(5):
                x0, x4 = F[c, i, 0], F[c, i, 4]
                F[c, i, 0] = x0 + jnp.where(bit_b == 1, roll_s(x4, 2), 0.0)
                F[c, i, 4] = x4 + jnp.where(bit_b == 0, roll_s(x0, -2), 0.0)

    def merge(x, y, bit, width, value):
        toward = width if value == 0 else -width
        return jnp.where(bit == value, x, roll_s(y, toward))

    def pack(comps, slot):
        for side in range(4):
            axis, value = side // 2, side % 2
            bit, width = ((bit_a, 1), (bit_b, 2))[axis]
            node = 4 * value
            buf = send[side]
            for c in range(comps):
                if axis == 0:
                    faces = [F[c, node, :, kp] for kp in range(3)]
                else:
                    faces = [F[c, :, node, kp] for kp in range(3)]
                buf[slot, c * 8 : c * 8 + 5] = merge(faces[0], faces[1], bit, width, value)
                z = faces[2]
                for n, (x, y) in enumerate(((0, 1), (2, 3), (4, 4))):
                    buf[slot, c * 8 + 5 + n : c * 8 + 6 + n] = merge(
                        z[x : x + 1], z[y : y + 1], bit, width, value
                    )
        for side in range(4, 8):
            da, db = SIDES[side]
            va, vb = (da + 1) // 2, (db + 1) // 2
            buf = send[side]
            for c in range(comps):
                x = F[c, 4 * va, 4 * vb]
                buf[slot, c : c + 1] = merge(x[0:1], x[1:2], bit_a, 1, va)
            for n in range((comps + 1) // 2):
                x = F[2 * n, 4 * va, 4 * vb, 2:3]
                y = F[min(2 * n + 1, comps - 1), 4 * va, 4 * vb, 2:3]
                buf[slot, comps + n : comps + n + 1] = merge(x, y, bit_a, 1, va)

    def unmerge(m, bit, width, value):
        toward = -width if value == 0 else width
        keep = bit == value
        return jnp.where(keep, roll_s(m, toward), 0.0), jnp.where(keep, m, 0.0)

    def unpack(comps, slot):
        for side in range(4):
            axis, value = side // 2, side % 2
            bit, width = ((bit_a, 1), (bit_b, 2))[axis]
            node = 4 * value
            buf = recv[side]
            for c in range(comps):
                adds = list(unmerge(buf[slot, c * 8 : c * 8 + 5], bit, width, value))
                pieces = []
                for n in range(3):
                    pieces.extend(
                        unmerge(buf[slot, c * 8 + 5 + n : c * 8 + 6 + n], bit, width, value)
                    )
                adds.append(jnp.concatenate(pieces[:5], axis=0))
                for kp in range(3):
                    if axis == 0:
                        F[c, node, :, kp] = F[c, node, :, kp] + adds[kp]
                    else:
                        F[c, :, node, kp] = F[c, :, node, kp] + adds[kp]
        for side in range(4, 8):
            da, db = SIDES[side]
            va, vb = (da + 1) // 2, (db + 1) // 2
            buf = recv[side]
            keep = bit_b == vb
            toward = -2 if vb == 0 else 2
            for n in range(message_rows(side, comps)):
                x, y = unmerge(buf[slot, n : n + 1], bit_a, 1, va)
                x = jnp.where(keep, roll_s(x, toward), 0.0)
                y = jnp.where(keep, roll_s(y, toward), 0.0)
                if n < comps:
                    at = [(n, 0, x), (n, 1, y)]
                else:
                    first = 2 * (n - comps)
                    at = [(first, 2, x)]
                    if first + 1 < comps:
                        at.append((first + 1, 2, y))
                for c, kp, v in at:
                    F[c, 4 * va, 4 * vb, kp : kp + 1] = F[c, 4 * va, 4 * vb, kp : kp + 1] + v

    def copy(side, comps, slot):
        rows = message_rows(side, comps)
        return pltpu.make_async_remote_copy(
            src_ref=send[side].at[slot, pl.ds(0, rows)],
            dst_ref=recv[OPPOSITE[side]].at[slot, pl.ds(0, rows)],
            send_sem=send_sem.at[side, slot],
            recv_sem=recv_sem.at[OPPOSITE[side], slot],
            device_id=target(side),
            device_id_type=MESH,
        )

    def arrival(side, comps, slot):
        rows = message_rows(side, comps)
        return pltpu.make_async_remote_copy(
            src_ref=send[side].at[slot, pl.ds(0, rows)],
            dst_ref=recv[side].at[slot, pl.ds(0, rows)],
            send_sem=send_sem.at[side, slot],
            recv_sem=recv_sem.at[side, slot],
            device_id=target(side),
            device_id_type=MESH,
        )

    def start(comps, slot):
        for side in range(8):

            @pl.when(exists(side))
            def _():
                copy(side, comps, slot).start()

    def finish(comps, slot):
        for side in range(8):

            @pl.when(exists(side))
            def _():
                arrival(side, comps, slot).wait()

    def quad(i, j):
        w = WEIGHTS
        scale = w[i] * w[j] / 8.0
        return jnp.concatenate(
            [half_row(scale * w[2 * kp], scale * w[min(2 * kp + 1, 4)], half) for kp in range(3)],
            axis=0,
        )

    def share(i, j):
        one = jnp.ones((1, 8, 128), F32)

        def along(n, bit, index, devices):
            if n == 0:
                return jnp.where((bit == 1) | (index > 0), 0.5, 1.0)
            if n == 4:
                return jnp.where((bit == 0) | (index < devices - 1), 0.5, 1.0)
            return one

        ab = along(i, bit_a, dom, nd) * along(j, bit_b, slab, ns)
        k0 = jnp.where((half == 0) & (lane > 0), 0.5, 1.0)
        k4 = jnp.where(lane < 127, 0.5, 1.0)
        return jnp.concatenate([ab * k0, ab * one, ab * k4], axis=0)

    load_pairs(U, disp)
    load_pairs(W, veloc)
    load_pairs(LAM, lame)
    load_pairs(MU, shear)
    load_pairs(CM, density)
    for i in range(5):
        for j in range(5):
            q = quad(i, j)
            F[3, i, j] = CM[i, j] * q
            LAM[i, j] = LAM[i, j] * q
            MU[i, j] = MU[i, j] * q
            for c in range(3):
                F[c, i, j] = U[c, i, j]
    local_sums(4)
    pack(4, 0)
    pl.semaphore_wait(barrier, count)
    start(4, 0)

    slots = got.shape[0]
    for k in range(CAP):
        block = got[:, k * 256 : (k + 1) * 256].astype(F32)
        TT[:, k * slots : (k + 1) * slots] = block.T
        el = block[:, EL : EL + 1] + 256.0 * block[:, EL + 1 : EL + 2]
        cols = lax.broadcasted_iota(jnp.int32, (slots, 512), 1)
        OH[k * slots : (k + 1) * slots, :] = (
            (cols == el.astype(jnp.int32)).astype(F32).astype(BF16)
        )

    def deposit(s):
        for c in range(3):
            row = c * STEPS + s
            src = TT[pl.ds(HI + row, 1), :] + TT[pl.ds(LO + row, 1), :]
            term = TT[0:152, :] * src
            high = term.astype(BF16)
            low = (term - high.astype(F32)).astype(BF16)
            sums = jnp.dot(high, OH[...], preferred_element_type=F32) + jnp.dot(
                low, OH[...], preferred_element_type=F32
            )
            for a in range(2):
                for b in range(2):
                    q, first = b * 2 + a, (a * 2 + b) * 128
                    DEP[pl.ds(c * 600 + q, NODES6, stride=4), :] = sums[
                        0:NODES6, first : first + 128
                    ]

    deposit(0)
    finish(4, 0)
    unpack(4, 0)
    for i in range(5):
        for j in range(5):
            part = share(i, j)
            mass = F[3, i, j]
            CM[i, j] = (DT * DT) / mass
            scaled = mass * part * (1.0 / DT)
            for c in range(3):
                U[c, i, j] = F[c, i, j] * part
                at = (c * 75 + (i * 5 + j) * 3) * 8
                DEP[at : at + 24, :] = DEP[at : at + 24, :] + (W[c, i, j] * scaled).reshape(
                    24, 128
                )
                W[c, i, j] = jnp.zeros((3, 8, 128), F32)

    pair = {(0, 0): 0, (1, 1): 1, (2, 2): 2, (0, 1): 3, (0, 2): 4, (1, 2): 5}

    def stress(c, d):
        return pair[(min(c, d), max(c, d))]

    def one_step(s, carry):
        for c in range(3):
            for j in range(5):
                outs = line(FORWARD, [U[c, i, j] for i in range(5)])
                for i in range(5):
                    GR[0, c, i, j] = outs[i]
            for i in range(5):
                outs = line(FORWARD, [U[c, i, j] for j in range(5)])
                for j in range(5):
                    GR[1, c, i, j] = outs[j]
                outs = kline(FORWARD, U[c, i, :, 0], U[c, i, :, 1], U[c, i, :, 2], half)
                for kp in range(3):
                    GR[2, c, i, :, kp] = outs[kp]
        for i in range(5):
            for j in range(5):
                g = [[GR[d, c, i, j] for c in range(3)] for d in range(3)]
                mu = MU[i, j]
                mu2 = mu + mu
                vol = LAM[i, j] * (g[0][0] + g[1][1] + g[2][2])
                for c in range(3):
                    SG[c, i, j] = mu2 * g[c][c] + vol
                    for d in range(c):
                        SG[stress(c, d), i, j] = mu * (g[c][d] + g[d][c])
        for c in range(3):
            for j in range(5):
                outs = line(BACKWARD, [SG[stress(c, 0), i, j] for i in range(5)])
                for i in range(5):
                    at = (c * 75 + (i * 5 + j) * 3) * 8
                    F[c, i, j] = outs[i] + DEP[at : at + 24, :].reshape(3, 8, 128)
            for i in range(5):
                outs = line(BACKWARD, [SG[stress(c, 1), i, j] for j in range(5)])
                for j in range(5):
                    F[c, i, j] = F[c, i, j] + outs[j]
                p = stress(c, 2)
                outs = kline(BACKWARD, SG[p, i, :, 0], SG[p, i, :, 1], SG[p, i, :, 2], half)
                for kp in range(3):
                    F[c, i, :, kp] = F[c, i, :, kp] + outs[kp]
        slot = (s + 1) % 2
        local_sums(3)
        pack(3, slot)
        start(3, slot)

        @pl.when(s < STEPS - 1)
        def _():
            deposit(s + 1)

        finish(3, slot)
        unpack(3, slot)
        for i in range(5):
            for j in range(5):
                cm = CM[i, j]
                for c in range(3):
                    w = W[c, i, j] + F[c, i, j] * cm
                    W[c, i, j] = w
                    U[c, i, j] = U[c, i, j] + w
        return carry

    lax.fori_loop(0, STEPS, one_step, 0)
    for i in range(5):
        for j in range(5):
            for c in range(3):
                W[c, i, j] = W[c, i, j] * (1.0 / DT)
    store_pairs(disp_out, U)
    store_pairs(veloc_out, W)


def to_rows(x):
    lead = x.shape[:-2]
    n = len(lead)
    y = x.reshape(lead + (2, 2, EC))
    return jnp.swapaxes(y, n, n + 1).reshape(lead + (4, EC))


def from_rows(x):
    lead = x.shape[:-2]
    n = len(lead)
    y = jnp.swapaxes(x.reshape(lead + (2, 2, EC)), n, n + 1)
    return y.reshape(lead + (2, 2 * EC))


def shards(
    nd,
    ns,
    displacement,
    velocity,
    lame_lambda,
    shear_modulus,
    density,
    traces,
    section_weights,
    owner,
    element_idx,
    node_weights,
    encode_bits,
):
    devices = nd * ns
    rows = traces.shape[0]
    payload = pl.pallas_call(
        functools.partial(pack_kernel, devices),
        out_shape=jax.ShapeDtypeStruct((devices, CAP * 256), BF16),
        scratch_shapes=[pltpu.VMEM((3, 128, section_weights.shape[1]), F32)],
        name="pack_rows",
    )(
        traces,
        section_weights,
        owner.reshape(1, rows),
        element_idx.reshape(1, rows),
        node_weights,
        encode_bits.T,
    )
    got = lax.all_to_all(payload, ("dom", "slab"), split_axis=0, concat_axis=0, tiled=True)
    field = (5, 5, 3, 8, 128)
    vm = lambda *shape: pltpu.VMEM(shape, F32)
    messages = [vm(2, message_rows(side, 4), 8, 128) for side in range(8)]
    out = jax.ShapeDtypeStruct((3, 5, 5, 5, 4, EC), F32)
    disp, veloc = pl.pallas_call(
        functools.partial(step_kernel, nd, ns),
        out_shape=(out, out),
        scratch_shapes=[
            vm(3, *field),
            vm(3, *field),
            vm(*field),
            vm(*field),
            vm(*field),
            vm(3, 3, *field),
            vm(6, *field),
            vm(4, *field),
            vm(1808, 128),
            vm(256, CAP * devices),
            pltpu.VMEM((CAP * devices, 512), BF16),
            *messages,
            *messages,
            pltpu.SemaphoreType.DMA((8, 2)),
            pltpu.SemaphoreType.DMA((8, 2)),
        ],
        compiler_params=pltpu.CompilerParams(collective_id=1, has_side_effects=True),
        name="time_steps",
    )(
        to_rows(displacement),
        to_rows(velocity),
        to_rows(lame_lambda),
        to_rows(shear_modulus),
        to_rows(density),
        got,
    )
    return from_rows(disp), from_rows(veloc)


def solution(mesh):
    nd, ns = mesh.shape["dom"], mesh.shape["slab"]
    both = P(("dom", "slab"), None)
    fields = P(None, None, None, None, "dom", "slab")
    params = P(None, None, None, "dom", "slab")
    return jax.shard_map(
        functools.partial(shards, nd, ns),
        mesh=mesh,
        in_specs=(
            fields,
            fields,
            params,
            params,
            params,
            both,
            P(),
            both,
            P(("dom", "slab")),
            both,
            both,
        ),
        out_specs=(fields, fields),
        check_vma=False,
    )
```

profile of v0, /device:TPU:23, one launch (start us, length us, event | category | flops | bytes accessed | tf_op | source)
XLA Modules:
  0.0 87.5 jit_solution(15364496753537894886)
XLA Ops:
  0.6 3.4 %pack_rows.1 = bf16[128,1024]{1,0:T(8,128)(2,1)} custom-call(bf16[256,3072]{1,0:T(8,128)(2,1)} %traces.1, bf16[4,256]{1,0:T(4,128)(2,1)} %weights.1, s32[1,256]{1,0:T(1,128)} %bitcast.52, s32[1,256]{1,0:T(1,128)} %bitcast.53, bf16[256,125]{1,0:T(8,128)(2,1)} %nodew.1, s32[4,256]{1,0:T(4,128)} %bitcast.51), custom_call_target="tpu_custom_call" | custom-call | tf_op jit(solution)/shard_map/pack_rows/pallas_call | solution.py:528
  4.0 0.5 broadcast
  4.6 1.7 %reduce = bf16[128,1024]{1,0:T(8,128)(2,1)S(1)} reduce(bf16[128,1,1024]{2,0,1:T(8,128)(2,1)} %bitcast.43, bf16[]{:T(256)} %broadcast), dimensions={1}, to_apply=%copy.33.reduce_sub_computation | reduce | bytes 524290 | tf_op jit(solution)/shard_map/all_to_all | solution.py:541
  6.3 0.2 reshape.70
  6.5 17.8 %all_to_all.11 = bf16[128,2,512]{2,1,0:T(2,128)(2,1)S(1)} all-to-all(bf16[128,2,512]{2,1,0:T(2,128)(2,1)S(1)} %reshape.70), channel_id=1, replica_groups=mesh['dom'=16,'slab'=8] {'dom','slab'}, dimensions={0} | all-to-all | bytes 524288 | tf_op jit(solution)/shard_map/all_to_all | solution.py:541
  24.2 0.2 reshape.71
  24.5 0.8 copy.38
  25.2 59.0 %time_steps.1 = (f32[3,5,5,5,4,128]{5,4,3,2,1,0:T(4,128)}, f32[3,5,5,5,4,128]{5,4,3,2,1,0:T(4,128)}) custom-call(f32[3,5,5,5,4,128]{5,4,3,2,1,0:T(4,128)} %bitcast.46, f32[3,5,5,5,4,128]{5,4,3,2,1,0:T(4,128)} %bitcast.47, f32[5,5,5,4,128]{4,3,2,1,0:T(4,128)} %bitcast.48, f32[5,5,5,4,128]{4,3,2,1,0:T(4,128)} %bitcast.49, f32[5,5,5,4,128]{4,3,2,1,0:T(4,128)} %bitcast.50, ...), custom_call_target="tpu_custom_call" | custom-call | tf_op jit(solution)/shard_map/time_steps/pallas_call | solution.py:546
  84.3 0.0 copy-start
  84.3 2.3 %copy.42 = f32[3,5,5,5,2,256]{5,4,3,2,1,0:T(2,128)} copy(f32[3,5,5,5,2,256]{5,4,3,2,1,0:T(2,128)} %bitcast.45) | data formatting | bytes 1536000
  86.6 0.0 copy-done
  86.6 0.9 copy.43
Async XLA Ops:
  84.3 2.3 %copy-start = (f32[3,5,5,5,4,128]{5,4,3,2,1,0:T(4,128)S(1)}, f32[3,5,5,5,4,128]{5,4,3,2,1,0:T(4,128)}, u32[]{:S(2)}) copy-start(f32[3,5,5,5,4,128]{5,4,3,2,1,0:T(4,128)} %get-tuple-element.5) | copy-start | bytes 2304004
where the time goes:
time: 87.7 us; the launch traced here: 87.5 us
  Pallas kernels  62.4 us (71%)
  blocking collectives  17.8 us (20%)
  local copies, waits for them, and re-layouts  4.91 us (6%)
  other arithmetic  1.72 us (2%)
    pallas_call x1, Pallas kernels, shards(): pl.pallas_call(functools.partial(step_kernel, nd, ns), out_shape=(out, ou...  59 us
    all_to_all x1, blocking collectives, shards(): lax.all_to_all(payload, ('dom', 'slab'), split_axis=0, concat_axis=0, til...  17.8 us
    unnamed x7, local copies, waits for them, and re-layouts  4.4 us
    pallas_call x1, Pallas kernels, shards(): pl.pallas_call(functools.partial(pack_kernel, devices), out_shape=jax.Sha...  3.41 us

commit v1 on v0

--- a/solution.py
+++ b/solution.py
@@ -130,10 +130,16 @@
 OPPOSITE = [1, 0, 3, 2, 7, 6, 5, 4]
 
 
-def message_rows(side, comps):
-    if side < 4:
-        return comps * 8
-    return comps + (comps + 1) // 2
+GROUPS = {3: ((0, 1, 2),), 4: ((0, 1, 2), (3,))}
+
+
+def tiles_of(group):
+    return (5 * len(group) + 2) // 2
+
+
+def sizes(comps):
+    groups = GROUPS[comps]
+    return sum(tiles_of(g) for g in groups), len(groups), (comps + 2) // 2
 
 
 def step_kernel(
@@ -161,7 +167,8 @@
     *rest,
 ):
     send, recv = rest[0:8], rest[8:16]
-    send_sem, recv_sem = rest[16], rest[17]
+    send_scale, recv_scale = rest[16:20], rest[20:24]
+    send_sem, recv_sem = rest[24], rest[25]
     dom, slab = lax.axis_index("dom"), lax.axis_index("slab")
 
     def exists(side):
@@ -178,6 +185,8 @@
 
     for side in range(8):
         recv[side][...] = jnp.zeros_like(recv[side])
+        if side < 4:
+            recv_scale[side][...] = jnp.zeros_like(recv_scale[side])
     barrier = pltpu.get_barrier_semaphore()
     count = 0
     for side in range(8):
@@ -213,9 +222,7 @@
         for c in range(comps):
             for i in range(5):
                 p0, p2 = F[c, i, :, 0], F[c, i, :, 2]
-                dup = jnp.where(half == 0, p0, roll_s(p0, 4))
                 F[c, i, :, 0] = p0 + jnp.where((half == 0) & (lane > 0), roll_l(p2, 1), 0.0)
-                F[c, i, :, 2] = p2 + jnp.where(lane < 127, roll_l(dup, -1), 0.0)
             for j in range(5):
                 x0, x4 = F[c, 0, j], F[c, 4, j]
                 F[c, 0, j] = x0 + jnp.where(bit_a == 1, roll_s(x4, 1), 0.0)
@@ -225,118 +232,142 @@
                 F[c, i, 0] = x0 + jnp.where(bit_b == 1, roll_s(x4, 2), 0.0)
                 F[c, i, 4] = x4 + jnp.where(bit_b == 0, roll_s(x0, -2), 0.0)
 
+    def close_k(x):
+        x0 = x[0:1]
+        dup = jnp.where(half == 0, x0, roll_s(x0, 4))
+        x2 = jnp.where(lane < 127, roll_l(dup, -1), x[2:3])
+        return jnp.concatenate([x[0:2], x2], axis=0)
+
     def merge(x, y, bit, width, value):
         toward = width if value == 0 else -width
         return jnp.where(bit == value, x, roll_s(y, toward))
-
-    def pack(comps, slot):
-        for side in range(4):
-            axis, value = side // 2, side % 2
-            bit, width = ((bit_a, 1), (bit_b, 2))[axis]
-            node = 4 * value
-            buf = send[side]
-            for c in range(comps):
-                if axis == 0:
-                    faces = [F[c, node, :, kp] for kp in range(3)]
-                else:
-                    faces = [F[c, :, node, kp] for kp in range(3)]
-                buf[slot, c * 8 : c * 8 + 5] = merge(faces[0], faces[1], bit, width, value)
-                z = faces[2]
-                for n, (x, y) in enumerate(((0, 1), (2, 3), (4, 4))):
-                    buf[slot, c * 8 + 5 + n : c * 8 + 6 + n] = merge(
-                        z[x : x + 1], z[y : y + 1], bit, width, value
-                    )
-        for side in range(4, 8):
-            da, db = SIDES[side]
-            va, vb = (da + 1) // 2, (db + 1) // 2
-            buf = send[side]
-            for c in range(comps):
-                x = F[c, 4 * va, 4 * vb]
-                buf[slot, c : c + 1] = merge(x[0:1], x[1:2], bit_a, 1, va)
-            for n in range((comps + 1) // 2):
-                x = F[2 * n, 4 * va, 4 * vb, 2:3]
-                y = F[min(2 * n + 1, comps - 1), 4 * va, 4 * vb, 2:3]
-                buf[slot, comps + n : comps + n + 1] = merge(x, y, bit_a, 1, va)
 
     def unmerge(m, bit, width, value):
         toward = -width if value == 0 else width
         keep = bit == value
         return jnp.where(keep, roll_s(m, toward), 0.0), jnp.where(keep, m, 0.0)
 
-    def unpack(comps, slot):
+    def ends(zs):
+        out = jnp.zeros((1, 8, 128), F32)
+        for n, z in enumerate(zs):
+            out = jnp.where(lane == n, roll_l(z, n + 1), out)
+        return out
+
+    def end_of(row, n):
+        return jnp.where(lane == 127, roll_l(row, 127 - n), 0.0)
+
+    def face(side):
+        axis, value = side // 2, side % 2
+        bit, width = ((bit_a, 1), (bit_b, 2))[axis]
+        node = 4 * value
+
+        def at(c, n, kp):
+            return (c, node, n, kp) if axis == 0 else (c, n, node, kp)
+
+        def line_at(c, kp):
+            return (c, node, slice(None), kp) if axis == 0 else (c, slice(None), node, kp)
+
+        return bit, width, value, at, line_at
+
+    def pack(comps, slot):
         for side in range(4):
-            axis, value = side // 2, side % 2
-            bit, width = ((bit_a, 1), (bit_b, 2))[axis]
-            node = 4 * value
-            buf = recv[side]
-            for c in range(comps):
-                adds = list(unmerge(buf[slot, c * 8 : c * 8 + 5], bit, width, value))
-                pieces = []
-                for n in range(3):
-                    pieces.extend(
-                        unmerge(buf[slot, c * 8 + 5 + n : c * 8 + 6 + n], bit, width, value)
-                    )
-                adds.append(jnp.concatenate(pieces[:5], axis=0))
-                for kp in range(3):
-                    if axis == 0:
-                        F[c, node, :, kp] = F[c, node, :, kp] + adds[kp]
-                    else:
-                        F[c, :, node, kp] = F[c, :, node, kp] + adds[kp]
+            bit, width, value, at, line_at = face(side)
+            tile = 0
+            for g, group in enumerate(GROUPS[comps]):
+                rows = []
+                for c in group:
+                    merged = merge(F[line_at(c, 0)], F[line_at(c, 1)], bit, width, value)
+                    rows.extend(merged[n : n + 1] for n in range(5))
+                rows.append(ends([F[at(c, n, 2)][None] for c in group for n in range(5)]))
+                largest = jnp.abs(rows[0])
+                for row in rows[1:]:
+                    largest = jnp.maximum(largest, jnp.abs(row))
+                scale = largest * (1.0 / 32000.0) + 1e-30
+                send_scale[side][slot, g : g + 1] = scale
+                inverse = 1.0 / scale
+                for n in range(0, len(rows), 2):
+                    x = jnp.concatenate([rows[n][0] * inverse[0], rows[n + 1][0] * inverse[0]], 0)
+                    x = x + jnp.where(x < 0.0, -0.5, 0.5)
+                    send[side][slot, tile] = x.astype(jnp.int32).astype(jnp.int16)
+                    tile += 1
         for side in range(4, 8):
             da, db = SIDES[side]
             va, vb = (da + 1) // 2, (db + 1) // 2
-            buf = recv[side]
-            keep = bit_b == vb
-            toward = -2 if vb == 0 else 2
-            for n in range(message_rows(side, comps)):
-                x, y = unmerge(buf[slot, n : n + 1], bit_a, 1, va)
-                x = jnp.where(keep, roll_s(x, toward), 0.0)
-                y = jnp.where(keep, roll_s(y, toward), 0.0)
-                if n < comps:
-                    at = [(n, 0, x), (n, 1, y)]
-                else:
-                    first = 2 * (n - comps)
-                    at = [(first, 2, x)]
-                    if first + 1 < comps:
-                        at.append((first + 1, 2, y))
-                for c, kp, v in at:
-                    F[c, 4 * va, 4 * vb, kp : kp + 1] = F[c, 4 * va, 4 * vb, kp : kp + 1] + v
-
-    def copy(side, comps, slot):
-        rows = message_rows(side, comps)
-        return pltpu.make_async_remote_copy(
-            src_ref=send[side].at[slot, pl.ds(0, rows)],
-            dst_ref=recv[OPPOSITE[side]].at[slot, pl.ds(0, rows)],
-            send_sem=send_sem.at[side, slot],
-            recv_sem=recv_sem.at[OPPOSITE[side], slot],
-            device_id=target(side),
-            device_id_type=MESH,
-        )
-
-    def arrival(side, comps, slot):
-        rows = message_rows(side, comps)
-        return pltpu.make_async_remote_copy(
-            src_ref=send[side].at[slot, pl.ds(0, rows)],
-            dst_ref=recv[side].at[slot, pl.ds(0, rows)],
-            send_sem=send_sem.at[side, slot],
-            recv_sem=recv_sem.at[side, slot],
-            device_id=target(side),
-            device_id_type=MESH,
-        )
+            items = []
+            for c in range(comps):
+                x = F[c, 4 * va, 4 * vb]
+                items.append(merge(x[0:1], x[1:2], bit_a, 1, va))
+            items.append(ends([F[c, 4 * va, 4 * vb, 2:3] for c in range(comps)]))
+            for n in range(0, len(items), 2):
+                y = items[min(n + 1, len(items) - 1)]
+                send[side][slot, n // 2 : n // 2 + 1] = merge(items[n], y, bit_b, 2, vb)
+
+    def unpack(comps, slot):
+        for side in range(4):
+            bit, width, value, at, line_at = face(side)
+            tile = 0
+            for g, group in enumerate(GROUPS[comps]):
+                scale = recv_scale[side][slot, g : g + 1]
+                rows = []
+                for _ in range(tiles_of(group)):
+                    x = recv[side][slot, tile].astype(jnp.int32).astype(F32)
+                    rows.extend([x[None, 0:8] * scale, x[None, 8:16] * scale])
+                    tile += 1
+                for m, c in enumerate(group):
+                    merged = jnp.concatenate(rows[5 * m : 5 * m + 5], axis=0)
+                    for kp, add in enumerate(unmerge(merged, bit, width, value)):
+                        F[line_at(c, kp)] = F[line_at(c, kp)] + add
+                last, _ = unmerge(rows[5 * len(group)], bit, width, value)
+                for m, c in enumerate(group):
+                    for n in range(5):
+                        F[at(c, n, 2)] = F[at(c, n, 2)] + end_of(last, 5 * m + n)[0]
+        for side in range(4, 8):
+            da, db = SIDES[side]
+            va, vb = (da + 1) // 2, (db + 1) // 2
+            items = []
+            for n in range(sizes(comps)[2]):
+                items.extend(unmerge(recv[side][slot, n : n + 1], bit_b, 2, vb))
+            last, _ = unmerge(items[comps], bit_a, 1, va)
+            for c in range(comps):
+                x, y = unmerge(items[c], bit_a, 1, va)
+                add = jnp.concatenate([x, y, end_of(last, c)], axis=0)
+                F[c, 4 * va, 4 * vb] = F[c, 4 * va, 4 * vb] + add
+
+    def copies(side, comps, slot, source):
+        tiles, scales, rows = sizes(comps)
+        parts = [(send, recv, tiles, side)] if side < 4 else [(send, recv, rows, side)]
+        if side < 4:
+            parts.append((send_scale, recv_scale, scales, 8 + side))
+        out = []
+        for src, dst, count, number in parts:
+            there = number - side + OPPOSITE[side] if source else number
+            out.append(
+                pltpu.make_async_remote_copy(
+                    src_ref=src[side].at[slot, pl.ds(0, count)],
+                    dst_ref=dst[OPPOSITE[side] if source else side].at[slot, pl.ds(0, count)],
+                    send_sem=send_sem.at[number, slot],
+                    recv_sem=recv_sem.at[there, slot],
+                    device_id=target(side),
+                    device_id_type=MESH,
+                )
+            )
+        return out
 
     def start(comps, slot):
-        for side in range(8):
+        for side in (0, 1, 2, 3, 4, 5, 6, 7):
 
             @pl.when(exists(side))
             def _():
-                copy(side, comps, slot).start()
+                for one in copies(side, comps, slot, True):
+                    one.start()
 
     def finish(comps, slot):
         for side in range(8):
 
             @pl.when(exists(side))
             def _():
-                arrival(side, comps, slot).wait()
+                for one in copies(side, comps, slot, False):
+                    one.wait()
 
     def quad(i, j):
         w = WEIGHTS
@@ -412,11 +443,11 @@
     for i in range(5):
         for j in range(5):
             part = share(i, j)
-            mass = F[3, i, j]
+            mass = close_k(F[3, i, j])
             CM[i, j] = (DT * DT) / mass
             scaled = mass * part * (1.0 / DT)
             for c in range(3):
-                U[c, i, j] = F[c, i, j] * part
+                U[c, i, j] = close_k(F[c, i, j]) * part
                 at = (c * 75 + (i * 5 + j) * 3) * 8
                 DEP[at : at + 24, :] = DEP[at : at + 24, :] + (W[c, i, j] * scaled).reshape(
                     24, 128
@@ -480,7 +511,7 @@
             for j in range(5):
                 cm = CM[i, j]
                 for c in range(3):
-                    w = W[c, i, j] + F[c, i, j] * cm
+                    w = W[c, i, j] + close_k(F[c, i, j]) * cm
                     W[c, i, j] = w
                     U[c, i, j] = U[c, i, j] + w
         return carry
@@ -489,7 +520,7 @@
     for i in range(5):
         for j in range(5):
             for c in range(3):
-                W[c, i, j] = W[c, i, j] * (1.0 / DT)
+                U[c, i, j] = U[c, i, j] - W[c, i, j]
     store_pairs(disp_out, U)
     store_pairs(veloc_out, W)
 
@@ -541,7 +572,10 @@
     got = lax.all_to_all(payload, ("dom", "slab"), split_axis=0, concat_axis=0, tiled=True)
     field = (5, 5, 3, 8, 128)
     vm = lambda *shape: pltpu.VMEM(shape, F32)
-    messages = [vm(2, message_rows(side, 4), 8, 128) for side in range(8)]
+    tiles, scales, ends = sizes(4)
+    messages = [pltpu.VMEM((2, tiles, 16, 128), jnp.int16) for side in range(4)]
+    messages += [vm(2, ends, 8, 128) for side in range(4)]
+    factors = [vm(2, scales, 8, 128) for side in range(4)]
     out = jax.ShapeDtypeStruct((3, 5, 5, 5, 4, EC), F32)
     disp, veloc = pl.pallas_call(
         functools.partial(step_kernel, nd, ns),
@@ -560,8 +594,10 @@
             pltpu.VMEM((CAP * devices, 512), BF16),
             *messages,
             *messages,
-            pltpu.SemaphoreType.DMA((8, 2)),
-            pltpu.SemaphoreType.DMA((8, 2)),
+            *factors,
+            *factors,
+            pltpu.SemaphoreType.DMA((12, 2)),
+            pltpu.SemaphoreType.DMA((12, 2)),
         ],
         compiler_params=pltpu.CompilerParams(collective_id=1, has_side_effects=True),
         name="time_steps",
@@ -573,7 +609,7 @@
         to_rows(density),
         got,
     )
-    return from_rows(disp), from_rows(veloc)
+    return from_rows(disp + veloc), from_rows(veloc * (1.0 / DT))
 
 
 def solution(mesh):

time: 87.7 us -> 69.9 us (0.80)
  the two profiles are of different devices: /device:TPU:23 before, /device:TPU:1 now
where the time goes in v1:
time: 69.9 us; the launch traced here: 69.6 us
  Pallas kernels  40.8 us (58%)
  blocking collectives  21.9 us (31%)
  other arithmetic  4.54 us (6%)
  local copies, waits for them, and re-layouts  1.7 us (2%)
    pallas_call x1, Pallas kernels, shards(): pl.pallas_call(functools.partial(step_kernel, nd, ns), out_shape=(out, ou...  37.4 us
    all_to_all x1, blocking collectives, shards(): lax.all_to_all(payload, ('dom', 'slab'), split_axis=0, concat_axis=0, til...  21.9 us
    pallas_call x1, Pallas kernels, shards(): pl.pallas_call(functools.partial(pack_kernel, devices), out_shape=jax.Sha...  3.41 us
    mul x1, other arithmetic, shards(): return (from_rows(disp + veloc), from_rows(veloc * (1.0 / DT)))  2.82 us
    all_to_all x1, other arithmetic, shards(): lax.all_to_all(payload, ('dom', 'slab'), split_axis=0, concat_axis=0, til...  1.72 us

profile of v1, /device:TPU:1, one launch (start us, length us, event | category | flops | bytes accessed | tf_op | source)
XLA Modules:
  0.0 69.6 jit_solution(868813181620825310)
XLA Ops:
  0.6 3.4 %pack_rows.1 = bf16[128,1024]{1,0:T(8,128)(2,1)} custom-call(bf16[256,3072]{1,0:T(8,128)(2,1)} %traces.1, bf16[4,256]{1,0:T(4,128)(2,1)} %weights.1, s32[1,256]{1,0:T(1,128)} %bitcast.52, s32[1,256]{1,0:T(1,128)} %bitcast.53, bf16[256,125]{1,0:T(8,128)(2,1)} %nodew.1, s32[4,256]{1,0:T(4,128)} %bitcast.51), custom_call_target="tpu_custom_call" | custom-call | tf_op jit(solution)/shard_map/pack_rows/pallas_call | solution.py:559
  4.0 0.5 broadcast
  4.6 1.7 %reduce = bf16[128,1024]{1,0:T(8,128)(2,1)S(1)} reduce(bf16[128,1,1024]{2,0,1:T(8,128)(2,1)} %bitcast.43, bf16[]{:T(256)} %broadcast), dimensions={1}, to_apply=%copy.33.reduce_sub_computation | reduce | bytes 524290 | tf_op jit(solution)/shard_map/all_to_all | solution.py:572
  6.3 0.2 reshape.70
  6.5 21.9 %all_to_all.11 = bf16[128,2,512]{2,1,0:T(2,128)(2,1)S(1)} all-to-all(bf16[128,2,512]{2,1,0:T(2,128)(2,1)S(1)} %reshape.70), channel_id=1, replica_groups=mesh['dom'=16,'slab'=8] {'dom','slab'}, dimensions={0} | all-to-all | bytes 524288 | tf_op jit(solution)/shard_map/all_to_all | solution.py:572
  28.3 0.2 reshape.71
  28.6 0.8 %copy.38 = bf16[128,1,1024]{2,0,1:T(8,128)(2,1)} copy(bf16[128,1,1024]{2,1,0:T(2,128)(2,1)S(1)} %reshape.71) | data formatting | bytes 524288
  29.4 37.4 %time_steps.1 = (f32[3,5,5,5,4,128]{5,4,3,2,1,0:T(4,128)}, f32[3,5,5,5,4,128]{5,4,3,2,1,0:T(4,128)}) custom-call(f32[3,5,5,5,4,128]{5,4,3,2,1,0:T(4,128)} %bitcast.46, f32[3,5,5,5,4,128]{5,4,3,2,1,0:T(4,128)} %bitcast.47, f32[5,5,5,4,128]{4,3,2,1,0:T(4,128)} %bitcast.48, f32[5,5,5,4,128]{4,3,2,1,0:T(4,128)} %bitcast.49, f32[5,5,5,4,128]{4,3,2,1,0:T(4,128)} %bitcast.50, ...), custom_call_target="tpu_custom_call" | custom-call | tf_op jit(solution)/shard_map/time_steps/pallas_call | solution.py:580
  66.8 2.8 %broadcast_multiply_fusion = (f32[3,5,5,5,4,128]{5,4,3,2,1,0:T(4,128)}, f32[3,5,5,5,4,128]{5,4,3,2,1,0:T(4,128)}) fusion(f32[3,5,5,5,4,128]{5,4,3,2,1,0:T(4,128)} %get-tuple-element.5, f32[3,5,5,5,4,128]{5,4,3,2,1,0:T(4,128)} %get-tuple-element.4), kind=kLoop, calls=%fused_computation | loop fusion | flops 384000 | bytes 3072000 | tf_op jit(solution)/shard_map/mul | solution.py:612

commit v2 on v1

--- a/solution.py
+++ b/solution.py
@@ -39,7 +39,7 @@
 FORWARD, BACKWARD = D2, -D2.T
 
 
-def pack_kernel(devices, traces, weights, owner, element, nodew, bits, out, wsel):
+def pack_rows(devices, traces, weights, owner, element, nodew, bits, out, wsel):
     rows = traces.shape[0]
     nt = weights.shape[1]
     signs = (2 * bits[...] - 1).astype(F32).T.astype(BF16)
@@ -85,7 +85,8 @@
     for k in range(CAP):
         choose = jnp.where(before == float(k), member, 0.0).astype(BF16)
         packed = jnp.dot(choose, right, preferred_element_type=F32)
-        out[:, k * 256 : (k + 1) * 256] = packed.astype(BF16)
+        out[pl.ds(k, devices, stride=8), :] = packed[:, :128]
+        out[pl.ds(CAP + k, devices, stride=8), :] = packed[:, 128:]
 
 
 def line(m, u):
@@ -150,9 +151,24 @@
     lame,
     shear,
     density,
-    got,
+    traces,
+    weights,
+    owner,
+    element,
+    nodew,
+    bits,
     disp_out,
     veloc_out,
+    raw_disp,
+    raw_veloc,
+    raw_lame,
+    raw_shear,
+    raw_density,
+    raw_traces,
+    WSEL,
+    ROWS,
+    OUT,
+    IN,
     U,
     W,
     LAM,
@@ -168,7 +184,7 @@
 ):
     send, recv = rest[0:8], rest[8:16]
     send_scale, recv_scale = rest[16:20], rest[20:24]
-    send_sem, recv_sem = rest[24], rest[25]
+    send_sem, recv_sem, load_sem, all_send, all_recv = rest[24:29]
     dom, slab = lax.axis_index("dom"), lax.axis_index("slab")
 
     def exists(side):
@@ -187,14 +203,69 @@
         recv[side][...] = jnp.zeros_like(recv[side])
         if side < 4:
             recv_scale[side][...] = jnp.zeros_like(recv_scale[side])
+    devices = nd * ns
+    me = dom * ns + slab
     barrier = pltpu.get_barrier_semaphore()
-    count = 0
-    for side in range(8):
-        count = count + exists(side).astype(jnp.int32)
-
-        @pl.when(exists(side))
-        def _():
-            pl.semaphore_signal(barrier, inc=1, device_id=target(side), device_id_type=MESH)
+
+    def other(step):
+        number = lax.rem(me + step, devices)
+        return number, (lax.div(number, ns), lax.rem(number, ns))
+
+    def greet(step, carry):
+        pl.semaphore_signal(barrier, inc=1, device_id=other(step)[1], device_id_type=MESH)
+        return carry
+
+    loads = [
+        pltpu.make_async_copy(src, dst, load_sem.at[n])
+        for n, (src, dst) in enumerate(
+            (
+                (traces, raw_traces),
+                (disp, raw_disp),
+                (density, raw_density),
+                (lame, raw_lame),
+                (shear, raw_shear),
+                (veloc, raw_veloc),
+            )
+        )
+    ]
+    for one in loads:
+        one.start()
+    lax.fori_loop(1, devices, greet, 0)
+
+    def row_copy(step):
+        number, there = other(step)
+        return pltpu.make_async_remote_copy(
+            src_ref=OUT.at[number],
+            dst_ref=IN.at[me],
+            send_sem=all_send,
+            recv_sem=all_recv,
+            device_id=there,
+            device_id_type=MESH,
+        )
+
+    def send_row(step, carry):
+        row_copy(step).start()
+        return carry
+
+    own_rows = pltpu.make_async_copy(OUT.at[me], IN.at[me], load_sem.at[6])
+
+    loads[0].wait()
+    pack_rows(devices, raw_traces, weights, owner, element, nodew, bits, ROWS, WSEL)
+    OUT[...] = ROWS[...].reshape(devices, 8, 128).astype(BF16)
+    pl.semaphore_wait(barrier, devices - 1)
+    own_rows.start()
+    lax.fori_loop(1, devices, send_row, 0)
+
+    def finish_rows():
+        own_rows.wait()
+        pltpu.make_async_remote_copy(
+            src_ref=OUT.at[pl.ds(0, devices - 1)],
+            dst_ref=IN.at[pl.ds(0, devices - 1)],
+            send_sem=all_send,
+            recv_sem=all_recv,
+            device_id=other(1)[1],
+            device_id_type=MESH,
+        ).wait()
 
     sub = lax.broadcasted_iota(jnp.int32, (1, 8, 128), 1)
     lane = lax.broadcasted_iota(jnp.int32, (1, 8, 128), 2)
@@ -218,10 +289,16 @@
             first = 4 * (k % 2)
             dst[lead + (k,)] = src[lead + (k // 2, slice(first, first + 4))]
 
-    def local_sums(comps):
+    def local_sums(comps, extra=None):
         for c in range(comps):
             for i in range(5):
-                p0, p2 = F[c, i, :, 0], F[c, i, :, 2]
+                p0, p1, p2 = (F[c, i, :, kp] for kp in range(3))
+                if extra is not None:
+                    at = (c * 75 + i * 15) * 8
+                    add = extra[at : at + 120, :].reshape(5, 3, 8, 128)
+                    p0, p2 = p0 + add[:, 0], p2 + add[:, 2]
+                    F[c, i, :, 1] = p1 + add[:, 1]
+                    F[c, i, :, 2] = p2
                 F[c, i, :, 0] = p0 + jnp.where((half == 0) & (lane > 0), roll_l(p2, 1), 0.0)
             for j in range(5):
                 x0, x4 = F[c, 0, j], F[c, 4, j]
@@ -270,7 +347,7 @@
         return bit, width, value, at, line_at
 
     def pack(comps, slot):
-        for side in range(4):
+        for side in (2, 3, 0, 1):
             bit, width, value, at, line_at = face(side)
             tile = 0
             for g, group in enumerate(GROUPS[comps]):
@@ -290,6 +367,7 @@
                     x = x + jnp.where(x < 0.0, -0.5, 0.5)
                     send[side][slot, tile] = x.astype(jnp.int32).astype(jnp.int16)
                     tile += 1
+            start(side, comps, slot)
         for side in range(4, 8):
             da, db = SIDES[side]
             va, vb = (da + 1) // 2, (db + 1) // 2
@@ -301,6 +379,7 @@
             for n in range(0, len(items), 2):
                 y = items[min(n + 1, len(items) - 1)]
                 send[side][slot, n // 2 : n // 2 + 1] = merge(items[n], y, bit_b, 2, vb)
+            start(side, comps, slot)
 
     def unpack(comps, slot):
         for side in range(4):
@@ -353,13 +432,11 @@
             )
         return out
 
-    def start(comps, slot):
-        for side in (0, 1, 2, 3, 4, 5, 6, 7):
-
-            @pl.when(exists(side))
-            def _():
-                for one in copies(side, comps, slot, True):
-                    one.start()
+    def start(side, comps, slot):
+        @pl.when(exists(side))
+        def _():
+            for one in copies(side, comps, slot, True):
+                one.start()
 
     def finish(comps, slot):
         for side in range(8):
@@ -392,33 +469,41 @@
         k4 = jnp.where(lane < 127, 0.5, 1.0)
         return jnp.concatenate([ab * k0, ab * one, ab * k4], axis=0)
 
-    load_pairs(U, disp)
-    load_pairs(W, veloc)
-    load_pairs(LAM, lame)
-    load_pairs(MU, shear)
-    load_pairs(CM, density)
+    loads[1].wait()
+    loads[2].wait()
+    load_pairs(U, raw_disp)
+    load_pairs(CM, raw_density)
     for i in range(5):
         for j in range(5):
-            q = quad(i, j)
-            F[3, i, j] = CM[i, j] * q
-            LAM[i, j] = LAM[i, j] * q
-            MU[i, j] = MU[i, j] * q
+            F[3, i, j] = CM[i, j] * quad(i, j)
             for c in range(3):
                 F[c, i, j] = U[c, i, j]
     local_sums(4)
     pack(4, 0)
-    pl.semaphore_wait(barrier, count)
-    start(4, 0)
-
-    slots = got.shape[0]
-    for k in range(CAP):
-        block = got[:, k * 256 : (k + 1) * 256].astype(F32)
-        TT[:, k * slots : (k + 1) * slots] = block.T
-        el = block[:, EL : EL + 1] + 256.0 * block[:, EL + 1 : EL + 2]
-        cols = lax.broadcasted_iota(jnp.int32, (slots, 512), 1)
-        OH[k * slots : (k + 1) * slots, :] = (
-            (cols == el.astype(jnp.int32)).astype(F32).astype(BF16)
-        )
+    for one in loads[3:]:
+        one.wait()
+    load_pairs(LAM, raw_lame)
+    load_pairs(MU, raw_shear)
+    load_pairs(W, raw_veloc)
+    for i in range(5):
+        for j in range(5):
+            q = quad(i, j)
+            LAM[i, j] = LAM[i, j] * q
+            MU[i, j] = MU[i, j] * q
+
+    def take_rows():
+        finish_rows()
+        ROWS[...] = IN[...].astype(F32).reshape(8 * devices, 128)
+        for k in range(CAP):
+            first = ROWS[pl.ds(k, devices, stride=8), :]
+            second = ROWS[pl.ds(CAP + k, devices, stride=8), :]
+            TT[0:128, k * devices : (k + 1) * devices] = first.T
+            TT[128:256, k * devices : (k + 1) * devices] = second.T
+            el = second[:, EL - 128 : EL - 127] + 256.0 * second[:, EL - 127 : EL - 126]
+            cols = lax.broadcasted_iota(jnp.int32, (devices, 512), 1)
+            OH[k * devices : (k + 1) * devices, :] = (
+                (cols == el.astype(jnp.int32)).astype(F32).astype(BF16)
+            )
 
     def deposit(s):
         for c in range(3):
@@ -437,7 +522,6 @@
                         0:NODES6, first : first + 128
                     ]
 
-    deposit(0)
     finish(4, 0)
     unpack(4, 0)
     for i in range(5):
@@ -448,11 +532,7 @@
             scaled = mass * part * (1.0 / DT)
             for c in range(3):
                 U[c, i, j] = close_k(F[c, i, j]) * part
-                at = (c * 75 + (i * 5 + j) * 3) * 8
-                DEP[at : at + 24, :] = DEP[at : at + 24, :] + (W[c, i, j] * scaled).reshape(
-                    24, 128
-                )
-                W[c, i, j] = jnp.zeros((3, 8, 128), F32)
+                W[c, i, j] = W[c, i, j] * scaled
 
     pair = {(0, 0): 0, (1, 1): 1, (2, 2): 2, (0, 1): 3, (0, 2): 4, (1, 2): 5}
 
@@ -486,8 +566,7 @@
             for j in range(5):
                 outs = line(BACKWARD, [SG[stress(c, 0), i, j] for i in range(5)])
                 for i in range(5):
-                    at = (c * 75 + (i * 5 + j) * 3) * 8
-                    F[c, i, j] = outs[i] + DEP[at : at + 24, :].reshape(3, 8, 128)
+                    F[c, i, j] = outs[i]
             for i in range(5):
                 outs = line(BACKWARD, [SG[stress(c, 1), i, j] for j in range(5)])
                 for j in range(5):
@@ -497,9 +576,19 @@
                 for kp in range(3):
                     F[c, i, :, kp] = F[c, i, :, kp] + outs[kp]
         slot = (s + 1) % 2
-        local_sums(3)
+
+        @pl.when(s == 0)
+        def _():
+            take_rows()
+            deposit(0)
+            for c in range(3):
+                for i in range(5):
+                    at = (c * 75 + i * 15) * 8
+                    DEP[at : at + 120, :] = DEP[at : at + 120, :] + W[c, i].reshape(120, 128)
+                    W[c, i] = jnp.zeros((5, 3, 8, 128), F32)
+
+        local_sums(3, DEP)
         pack(3, slot)
-        start(3, slot)
 
         @pl.when(s < STEPS - 1)
         def _():
@@ -556,20 +645,6 @@
 ):
     devices = nd * ns
     rows = traces.shape[0]
-    payload = pl.pallas_call(
-        functools.partial(pack_kernel, devices),
-        out_shape=jax.ShapeDtypeStruct((devices, CAP * 256), BF16),
-        scratch_shapes=[pltpu.VMEM((3, 128, section_weights.shape[1]), F32)],
-        name="pack_rows",
-    )(
-        traces,
-        section_weights,
-        owner.reshape(1, rows),
-        element_idx.reshape(1, rows),
-        node_weights,
-        encode_bits.T,
-    )
-    got = lax.all_to_all(payload, ("dom", "slab"), split_axis=0, concat_axis=0, tiled=True)
     field = (5, 5, 3, 8, 128)
     vm = lambda *shape: pltpu.VMEM(shape, F32)
     tiles, scales, ends = sizes(4)
@@ -580,7 +655,20 @@
     disp, veloc = pl.pallas_call(
         functools.partial(step_kernel, nd, ns),
         out_shape=(out, out),
+        in_specs=[pl.BlockSpec(memory_space=pl.ANY)] * 6
+        + [pl.BlockSpec(memory_space=pltpu.VMEM)] * 5,
+        out_specs=(pl.BlockSpec(memory_space=pltpu.VMEM),) * 2,
         scratch_shapes=[
+            vm(3, 5, 5, 5, 4, EC),
+            vm(3, 5, 5, 5, 4, EC),
+            vm(5, 5, 5, 4, EC),
+            vm(5, 5, 5, 4, EC),
+            vm(5, 5, 5, 4, EC),
+            pltpu.VMEM(traces.shape, BF16),
+            vm(3, 128, section_weights.shape[1]),
+            vm(8 * devices, 128),
+            pltpu.VMEM((devices, 8, 128), BF16),
+            pltpu.VMEM((devices, 8, 128), BF16),
             vm(3, *field),
             vm(3, *field),
             vm(*field),
@@ -598,6 +686,9 @@
             *factors,
             pltpu.SemaphoreType.DMA((12, 2)),
             pltpu.SemaphoreType.DMA((12, 2)),
+            pltpu.SemaphoreType.DMA((7,)),
+            pltpu.SemaphoreType.DMA,
+            pltpu.SemaphoreType.DMA,
         ],
         compiler_params=pltpu.CompilerParams(collective_id=1, has_side_effects=True),
         name="time_steps",
@@ -607,7 +698,12 @@
         to_rows(lame_lambda),
         to_rows(shear_modulus),
         to_rows(density),
-        got,
+        traces,
+        section_weights,
+        owner.reshape(1, rows),
+        element_idx.reshape(1, rows),
+        node_weights,
+        encode_bits.T,
     )
     return from_rows(disp + veloc), from_rows(veloc * (1.0 / DT))
 

time: 69.9 us -> 55.6 us (0.80)
  the two profiles are of different devices: /device:TPU:1 before, /device:TPU:6 now
where the time goes in v2:
time: 55.6 us; the launch traced here: 55.4 us
  Pallas kernels  51.9 us (93%)
  other arithmetic  2.82 us (5%)
  between operations  0.64 us (1%)
    pallas_call x1, Pallas kernels, shards(): pl.pallas_call(functools.partial(step_kernel, nd, ns), out_shape=(out, ou...  51.9 us
    mul x1, other arithmetic, shards(): return (from_rows(disp + veloc), from_rows(veloc * (1.0 / DT)))  2.82 us

profile of v2, /device:TPU:6, one launch (start us, length us, event | category | flops | bytes accessed | tf_op | source)
XLA Modules:
  0.0 55.4 jit_solution(15145129174773815463)
XLA Ops:
  0.6 51.9 %time_steps.1 = (f32[3,5,5,5,4,128]{5,4,3,2,1,0:T(4,128)}, f32[3,5,5,5,4,128]{5,4,3,2,1,0:T(4,128)}) custom-call(f32[3,5,5,5,4,128]{5,4,3,2,1,0:T(4,128)} %bitcast.38, f32[3,5,5,5,4,128]{5,4,3,2,1,0:T(4,128)} %bitcast.39, f32[5,5,5,4,128]{4,3,2,1,0:T(4,128)} %bitcast.42, f32[5,5,5,4,128]{4,3,2,1,0:T(4,128)} %bitcast.43, f32[5,5,5,4,128]{4,3,2,1,0:T(4,128)} %bitcast.44, ...), custom_call_target="tpu_custom_call" | custom-call | tf_op jit(solution)/shard_map/time_steps/pallas_call | solution.py:655
  52.6 2.8 %broadcast_multiply_fusion = (f32[3,5,5,5,4,128]{5,4,3,2,1,0:T(4,128)}, f32[3,5,5,5,4,128]{5,4,3,2,1,0:T(4,128)}) fusion(f32[3,5,5,5,4,128]{5,4,3,2,1,0:T(4,128)} %get-tuple-element.5, f32[3,5,5,5,4,128]{5,4,3,2,1,0:T(4,128)} %get-tuple-element.4), kind=kLoop, calls=%fused_computation | loop fusion | flops 384000 | bytes 3072000 | tf_op jit(solution)/shard_map/mul | solution.py:708

commit v3 on v2

--- a/solution.py
+++ b/solution.py
@@ -39,41 +39,16 @@
 FORWARD, BACKWARD = D2, -D2.T
 
 
-def pack_rows(devices, traces, weights, owner, element, nodew, bits, out, wsel):
-    rows = traces.shape[0]
-    nt = weights.shape[1]
-    signs = (2 * bits[...] - 1).astype(F32).T.astype(BF16)
+def choose_rows(devices, weights, owner, nodew, choose, wide, wsel):
+    rows = nodew.shape[0]
     wsel[...] = jnp.zeros_like(wsel)
     for c in range(3):
         wsel[c, c * STEPS : (c + 1) * STEPS, :] = weights[...].astype(F32)
-    source = jnp.zeros((rows, 128), F32)
-    for g in range(G):
-        sign = signs[:, g : g + 1]
-        for c in range(3):
-            first = (g * 3 + c) * nt
-            block = traces[:, first : first + nt] * sign
-            source = source + lax.dot_general(
-                block,
-                wsel[c].astype(BF16),
-                (((1,), (1,)), ((), ())),
-                preferred_element_type=F32,
-            )
-    high = source.astype(BF16).astype(F32)
-    low = source - high
-    lane = lax.broadcasted_iota(jnp.int32, (rows, 128), 1)
-    where_el = jnp.broadcast_to(element[...], (128, rows)).astype(F32).T
-    el_high = jnp.floor(where_el * (1.0 / 256.0))
-    el_low = where_el - 256.0 * el_high
-    base = HI - 128
-    extra = pltpu.roll(high, base, 1) + pltpu.roll(low, LO - 128, 1)
-    extra = jnp.where(lane == EL - 128, el_low, extra)
-    extra = jnp.where(lane == EL - 127, el_high, extra)
     node = lax.broadcasted_iota(jnp.int32, (125, 256), 0)
     column = lax.broadcasted_iota(jnp.int32, (125, 256), 1)
     slot6 = (node // 5) * 6 + node % 5
     spread = (column == slot6) | ((node % 5 == 4) & (column == slot6 + 1))
-    wide = jnp.dot(nodew[...], spread.astype(F32).astype(BF16), preferred_element_type=F32)
-    right = jnp.concatenate([wide[:, :128], wide[:, 128:] + extra], axis=1).astype(BF16)
+    wide[...] = jnp.dot(nodew[...], spread.astype(F32).astype(BF16), preferred_element_type=F32)
     device = lax.broadcasted_iota(jnp.int32, (devices, rows), 0)
     member = (owner[...] == device).astype(F32)
     earlier = lax.broadcasted_iota(jnp.int32, (rows, rows), 0) < lax.broadcasted_iota(
@@ -83,10 +58,49 @@
         member.astype(BF16), earlier.astype(F32).astype(BF16), preferred_element_type=F32
     )
     for k in range(CAP):
-        choose = jnp.where(before == float(k), member, 0.0).astype(BF16)
-        packed = jnp.dot(choose, right, preferred_element_type=F32)
-        out[pl.ds(k, devices, stride=8), :] = packed[:, :128]
-        out[pl.ds(CAP + k, devices, stride=8), :] = packed[:, 128:]
+        choose[k] = jnp.where(before == float(k), member, 0.0).astype(BF16)
+
+
+def pack_first(devices, choose, wide, out):
+    right = wide[:, :128].astype(BF16)
+    for k in range(CAP):
+        out[pl.ds(k, devices, stride=8), :] = jnp.dot(
+            choose[k], right, preferred_element_type=F32
+        )
+
+
+def pack_second(devices, traces, element, bits, choose, wide, wsel, out):
+    rows = traces.shape[0]
+    nt = wsel.shape[2]
+    signs = (2 * bits[...] - 1).astype(F32).T.astype(BF16)
+    sources = []
+    for c in range(3):
+        source = jnp.zeros((rows, 128), F32)
+        for g in range(G):
+            first = (g * 3 + c) * nt
+            block = traces[:, first : first + nt] * signs[:, g : g + 1]
+            source = source + lax.dot_general(
+                block,
+                wsel[c].astype(BF16),
+                (((1,), (1,)), ((), ())),
+                preferred_element_type=F32,
+            )
+        sources.append(source)
+    source = sources[0] + sources[1] + sources[2]
+    high = source.astype(BF16).astype(F32)
+    low = source - high
+    lane = lax.broadcasted_iota(jnp.int32, (rows, 128), 1)
+    where_el = jnp.broadcast_to(element[...], (128, rows)).astype(F32).T
+    el_high = jnp.floor(where_el * (1.0 / 256.0))
+    el_low = where_el - 256.0 * el_high
+    extra = pltpu.roll(high, HI - 128, 1) + pltpu.roll(low, LO - 128, 1)
+    extra = jnp.where(lane == EL - 128, el_low, extra)
+    extra = jnp.where(lane == EL - 127, el_high, extra)
+    right = (wide[:, 128:] + extra).astype(BF16)
+    for k in range(CAP):
+        out[pl.ds(CAP + k, devices, stride=8), :] = jnp.dot(
+            choose[k], right, preferred_element_type=F32
+        )
 
 
 def line(m, u):
@@ -138,6 +152,26 @@
     return (5 * len(group) + 2) // 2
 
 
+def far_first(nd, ns):
+    zs = max(nd // 4, 1)
+
+    def ring(d, n):
+        return min(d % n, -d % n)
+
+    def way(k, j):
+        total = 0
+        for d in range(nd):
+            e = (d + k) % nd
+            total += ns * (2 * (d // (2 * zs) != e // (2 * zs)) + ring(d // 2 - e // 2, zs))
+        for b in range(ns):
+            e = (b + j) % ns
+            total += nd * (ring(b // 2 - e // 2, max(ns // 2, 1)) + (b % 2 != e % 2))
+        return total
+
+    steps = [(k, j) for k in range(nd) for j in range(ns) if (k, j) != (0, 0)]
+    return sorted(steps, key=lambda step: (-way(*step), step))
+
+
 def sizes(comps):
     groups = GROUPS[comps]
     return sum(tiles_of(g) for g in groups), len(groups), (comps + 2) // 2
@@ -152,19 +186,26 @@
     shear,
     density,
     traces,
+    weights_in,
+    owner_in,
+    element_in,
+    nodew_in,
+    bits_in,
+    disp_out,
+    veloc_out,
     weights,
     owner,
     element,
     nodew,
     bits,
-    disp_out,
-    veloc_out,
     raw_disp,
     raw_veloc,
     raw_lame,
     raw_shear,
     raw_density,
     raw_traces,
+    CHOOSE,
+    WIDE,
     WSEL,
     ROWS,
     OUT,
@@ -207,13 +248,9 @@
     me = dom * ns + slab
     barrier = pltpu.get_barrier_semaphore()
 
-    def other(step):
-        number = lax.rem(me + step, devices)
-        return number, (lax.div(number, ns), lax.rem(number, ns))
-
-    def greet(step, carry):
-        pl.semaphore_signal(barrier, inc=1, device_id=other(step)[1], device_id_type=MESH)
-        return carry
+    doms = [lax.rem(dom + k, nd) for k in range(nd)]
+    slabs = [lax.rem(slab + k, ns) for k in range(ns)]
+    order = far_first(nd, ns)
 
     loads = [
         pltpu.make_async_copy(src, dst, load_sem.at[n])
@@ -228,44 +265,59 @@
             )
         )
     ]
-    for one in loads:
+    small = [
+        pltpu.make_async_copy(src, dst, load_sem.at[7 + n])
+        for n, (src, dst) in enumerate(
+            (
+                (owner_in, owner),
+                (nodew_in, nodew),
+                (weights_in, weights),
+                (bits_in, bits),
+                (element_in, element),
+            )
+        )
+    ]
+    for one in small + loads[:3]:
         one.start()
-    lax.fori_loop(1, devices, greet, 0)
-
-    def row_copy(step):
-        number, there = other(step)
-        return pltpu.make_async_remote_copy(
-            src_ref=OUT.at[number],
-            dst_ref=IN.at[me],
-            send_sem=all_send,
-            recv_sem=all_recv,
-            device_id=there,
-            device_id_type=MESH,
+    for k, j in order:
+        pl.semaphore_signal(
+            barrier, inc=1, device_id=(doms[k], slabs[j]), device_id_type=MESH
         )
-
-    def send_row(step, carry):
-        row_copy(step).start()
-        return carry
-
     own_rows = pltpu.make_async_copy(OUT.at[me], IN.at[me], load_sem.at[6])
 
-    loads[0].wait()
-    pack_rows(devices, raw_traces, weights, owner, element, nodew, bits, ROWS, WSEL)
-    OUT[...] = ROWS[...].reshape(devices, 8, 128).astype(BF16)
-    pl.semaphore_wait(barrier, devices - 1)
-    own_rows.start()
-    lax.fori_loop(1, devices, send_row, 0)
+    def send_rows():
+        own_rows.start()
+        for k, j in order:
+            pltpu.make_async_remote_copy(
+                src_ref=OUT.at[doms[k] * ns + slabs[j]],
+                dst_ref=IN.at[me],
+                send_sem=all_send,
+                recv_sem=all_recv,
+                device_id=(doms[k], slabs[j]),
+                device_id_type=MESH,
+            ).start()
 
     def finish_rows():
         own_rows.wait()
+        k, j = order[0]
         pltpu.make_async_remote_copy(
             src_ref=OUT.at[pl.ds(0, devices - 1)],
             dst_ref=IN.at[pl.ds(0, devices - 1)],
             send_sem=all_send,
             recv_sem=all_recv,
-            device_id=other(1)[1],
+            device_id=(doms[k], slabs[j]),
             device_id_type=MESH,
         ).wait()
+
+    for one in small:
+        one.wait()
+    choose_rows(devices, weights, owner, nodew, CHOOSE, WIDE, WSEL)
+    pack_first(devices, CHOOSE, WIDE, ROWS)
+    loads[0].wait()
+    for one in loads[3:]:
+        one.start()
+    pack_second(devices, raw_traces, element, bits, CHOOSE, WIDE, WSEL, ROWS)
+    OUT[...] = ROWS[...].reshape(devices, 8, 128).astype(BF16)
 
     sub = lax.broadcasted_iota(jnp.int32, (1, 8, 128), 1)
     lane = lax.broadcasted_iota(jnp.int32, (1, 8, 128), 2)
@@ -347,7 +399,7 @@
         return bit, width, value, at, line_at
 
     def pack(comps, slot):
-        for side in (2, 3, 0, 1):
+        for side in (0, 1, 2, 3):
             bit, width, value, at, line_at = face(side)
             tile = 0
             for g, group in enumerate(GROUPS[comps]):
@@ -382,7 +434,8 @@
             start(side, comps, slot)
 
     def unpack(comps, slot):
-        for side in range(4):
+        for side in (2, 3, 0, 1):
+            finish(side, comps, slot)
             bit, width, value, at, line_at = face(side)
             tile = 0
             for g, group in enumerate(GROUPS[comps]):
@@ -404,6 +457,7 @@
             da, db = SIDES[side]
             va, vb = (da + 1) // 2, (db + 1) // 2
             items = []
+            finish(side, comps, slot)
             for n in range(sizes(comps)[2]):
                 items.extend(unmerge(recv[side][slot, n : n + 1], bit_b, 2, vb))
             last, _ = unmerge(items[comps], bit_a, 1, va)
@@ -438,13 +492,11 @@
             for one in copies(side, comps, slot, True):
                 one.start()
 
-    def finish(comps, slot):
-        for side in range(8):
-
-            @pl.when(exists(side))
-            def _():
-                for one in copies(side, comps, slot, False):
-                    one.wait()
+    def finish(side, comps, slot):
+        @pl.when(exists(side))
+        def _():
+            for one in copies(side, comps, slot, False):
+                one.wait()
 
     def quad(i, j):
         w = WEIGHTS
@@ -479,6 +531,8 @@
             for c in range(3):
                 F[c, i, j] = U[c, i, j]
     local_sums(4)
+    pl.semaphore_wait(barrier, devices - 1)
+    send_rows()
     pack(4, 0)
     for one in loads[3:]:
         one.wait()
@@ -522,7 +576,6 @@
                         0:NODES6, first : first + 128
                     ]
 
-    finish(4, 0)
     unpack(4, 0)
     for i in range(5):
         for j in range(5):
@@ -594,16 +647,19 @@
         def _():
             deposit(s + 1)
 
-        finish(3, slot)
+        inner = [(i, j) for i in range(1, 4) for j in range(1, 4)]
+        update(inner)
         unpack(3, slot)
-        for i in range(5):
-            for j in range(5):
-                cm = CM[i, j]
-                for c in range(3):
-                    w = W[c, i, j] + close_k(F[c, i, j]) * cm
-                    W[c, i, j] = w
-                    U[c, i, j] = U[c, i, j] + w
+        update([(i, j) for i in range(5) for j in range(5) if (i, j) not in inner])
         return carry
+
+    def update(lines):
+        for i, j in lines:
+            cm = CM[i, j]
+            for c in range(3):
+                w = W[c, i, j] + close_k(F[c, i, j]) * cm
+                W[c, i, j] = w
+                U[c, i, j] = U[c, i, j] + w
 
     lax.fori_loop(0, STEPS, one_step, 0)
     for i in range(5):
@@ -655,16 +711,22 @@
     disp, veloc = pl.pallas_call(
         functools.partial(step_kernel, nd, ns),
         out_shape=(out, out),
-        in_specs=[pl.BlockSpec(memory_space=pl.ANY)] * 6
-        + [pl.BlockSpec(memory_space=pltpu.VMEM)] * 5,
+        in_specs=[pl.BlockSpec(memory_space=pltpu.HBM)] * 11,
         out_specs=(pl.BlockSpec(memory_space=pltpu.VMEM),) * 2,
         scratch_shapes=[
+            pltpu.VMEM(section_weights.shape, BF16),
+            pltpu.VMEM((1, rows), jnp.int32),
+            pltpu.VMEM((1, rows), jnp.int32),
+            pltpu.VMEM(node_weights.shape, BF16),
+            pltpu.VMEM((G, rows), jnp.int32),
             vm(3, 5, 5, 5, 4, EC),
             vm(3, 5, 5, 5, 4, EC),
             vm(5, 5, 5, 4, EC),
             vm(5, 5, 5, 4, EC),
             vm(5, 5, 5, 4, EC),
             pltpu.VMEM(traces.shape, BF16),
+            pltpu.VMEM((CAP, devices, rows), BF16),
+            vm(rows, 256),
             vm(3, 128, section_weights.shape[1]),
             vm(8 * devices, 128),
             pltpu.VMEM((devices, 8, 128), BF16),
@@ -686,24 +748,31 @@
             *factors,
             pltpu.SemaphoreType.DMA((12, 2)),
             pltpu.SemaphoreType.DMA((12, 2)),
-            pltpu.SemaphoreType.DMA((7,)),
+            pltpu.SemaphoreType.DMA((12,)),
             pltpu.SemaphoreType.DMA,
             pltpu.SemaphoreType.DMA,
         ],
-        compiler_params=pltpu.CompilerParams(collective_id=1, has_side_effects=True),
+        compiler_params=pltpu.CompilerParams(
+            collective_id=1, has_side_effects=True, vmem_limit_bytes=28 * 2**20
+        ),
         name="time_steps",
     )(
-        to_rows(displacement),
-        to_rows(velocity),
-        to_rows(lame_lambda),
-        to_rows(shear_modulus),
-        to_rows(density),
-        traces,
-        section_weights,
-        owner.reshape(1, rows),
-        element_idx.reshape(1, rows),
-        node_weights,
-        encode_bits.T,
+        *(
+            pltpu.with_memory_space_constraint(x, pltpu.HBM)
+            for x in (
+                to_rows(displacement),
+                to_rows(velocity),
+                to_rows(lame_lambda),
+                to_rows(shear_modulus),
+                to_rows(density),
+                traces,
+                section_weights,
+                owner.reshape(1, rows),
+                element_idx.reshape(1, rows),
+                node_weights,
+                encode_bits.T,
+            )
+        )
     )
     return from_rows(disp + veloc), from_rows(veloc * (1.0 / DT))
 

time: 55.6 us -> 49.4 us (0.89)
  Pallas kernels: 51.9 us -> 47.2 us
  other arithmetic: 2.82 us -> 1.46 us
    pallas_call x1, Pallas kernels: 51.9 us -> 47.2 us  [shards(): pl.pallas_call(functools.partial(step_kernel, nd, ns), out_shape=(out, ou...]
    mul x1, other arithmetic: 2.82 us -> 1.46 us  [shards(): return (from_rows(disp + veloc), from_rows(veloc * (1.0 / DT)))]
where the time goes in v3:
time: 49.4 us; the launch traced here: 49.3 us
  Pallas kernels  47.2 us (96%)
  other arithmetic  1.46 us (3%)
  between operations  0.64 us (1%)
    pallas_call x1, Pallas kernels, shards(): pl.pallas_call(functools.partial(step_kernel, nd, ns), out_shape=(out, ou...  47.2 us
    mul x1, other arithmetic, shards(): return (from_rows(disp + veloc), from_rows(veloc * (1.0 / DT)))  1.46 us

profile of v3, /device:TPU:6, one launch (start us, length us, event | category | flops | bytes accessed | tf_op | source)
XLA Modules:
  0.0 49.3 jit_solution(12986287376215033081)
XLA Ops:
  0.6 47.2 %time_steps.1 = (f32[3,5,5,5,4,128]{5,4,3,2,1,0:T(4,128)S(1)}, f32[3,5,5,5,4,128]{5,4,3,2,1,0:T(4,128)S(1)}) custom-call(f32[3,5,5,5,4,128]{5,4,3,2,1,0:T(4,128)} %bitcast.38, f32[3,5,5,5,4,128]{5,4,3,2,1,0:T(4,128)} %bitcast.39, f32[5,5,5,4,128]{4,3,2,1,0:T(4,128)} %bitcast.42, f32[5,5,5,4,128]{4,3,2,1,0:T(4,128)} %bitcast.43, ...), custom_call_target="tpu_custom_call" | custom-call | tf_op jit(solution)/shard_map/time_steps/pallas_call | solution.py:711
  47.9 1.5 %broadcast_multiply_fusion = (f32[3,5,5,5,4,128]{5,4,3,2,1,0:T(4,128)}, f32[3,5,5,5,4,128]{5,4,3,2,1,0:T(4,128)}) fusion(f32[3,5,5,5,4,128]{5,4,3,2,1,0:T(4,128)S(1)} %get-tuple-element.5, f32[3,5,5,5,4,128]{5,4,3,2,1,0:T(4,128)S(1)} %get-tuple-element.4), kind=kLoop, calls=%fused_computation | loop fusion | flops 384000 | bytes 3072000 | tf_op jit(solution)/shard_map/mul | solution.py:777

commit v4 on v3

--- a/solution.py
+++ b/solution.py
@@ -103,16 +103,19 @@
         )
 
 
-def line(m, u):
+def line(m, u, wanted=(0, 1, 2, 3, 4)):
     e0, e1, o0, o1 = u[0] + u[4], u[1] + u[3], u[0] - u[4], u[1] - u[3]
-    even, odd = [], []
+    out = {}
     for i in range(2):
-        ce = [float((m[i, l] + m[i, 4 - l]) / 2) for l in range(2)]
-        co = [float((m[i, l] - m[i, 4 - l]) / 2) for l in range(2)]
-        even.append(ce[0] * e0 + ce[1] * e1 + float(m[i, 2]) * u[2])
-        odd.append(co[0] * o0 + co[1] * o1)
-    middle = float(m[2, 0]) * o0 + float(m[2, 1]) * o1
-    return [even[0] + odd[0], even[1] + odd[1], middle, odd[1] - even[1], odd[0] - even[0]]
+        if i in wanted or 4 - i in wanted:
+            ce = [float((m[i, l] + m[i, 4 - l]) / 2) for l in range(2)]
+            co = [float((m[i, l] - m[i, 4 - l]) / 2) for l in range(2)]
+            even = ce[0] * e0 + ce[1] * e1 + float(m[i, 2]) * u[2]
+            odd = co[0] * o0 + co[1] * o1
+            out[i], out[4 - i] = odd + even, odd - even
+    if 2 in wanted:
+        out[2] = float(m[2, 0]) * o0 + float(m[2, 1]) * o1
+    return out
 
 
 def half_row(lower, upper, half):
@@ -143,6 +146,7 @@
 
 SIDES = [(-1, 0), (1, 0), (0, -1), (0, 1), (-1, -1), (-1, 1), (1, -1), (1, 1)]
 OPPOSITE = [1, 0, 3, 2, 7, 6, 5, 4]
+ENDS, SLABS = (0, 1, 4, 5, 6, 7), (2, 3)
 
 
 GROUPS = {3: ((0, 1, 2),), 4: ((0, 1, 2), (3,))}
@@ -241,9 +245,13 @@
         return (dom + SIDES[side][0], slab + SIDES[side][1])
 
     for side in range(8):
-        recv[side][...] = jnp.zeros_like(recv[side])
-        if side < 4:
-            recv_scale[side][...] = jnp.zeros_like(recv_scale[side])
+
+        @pl.when(jnp.logical_not(exists(side)))
+        def _():
+            recv[side][...] = jnp.zeros_like(recv[side])
+            if side < 4:
+                recv_scale[side][...] = jnp.zeros_like(recv_scale[side])
+
     devices = nd * ns
     me = dom * ns + slab
     barrier = pltpu.get_barrier_semaphore()
@@ -341,9 +349,9 @@
             first = 4 * (k % 2)
             dst[lead + (k,)] = src[lead + (k // 2, slice(first, first + 4))]
 
-    def local_sums(comps, extra=None):
+    def local_sums(comps, planes, extra=None):
         for c in range(comps):
-            for i in range(5):
+            for i in planes:
                 p0, p1, p2 = (F[c, i, :, kp] for kp in range(3))
                 if extra is not None:
                     at = (c * 75 + i * 15) * 8
@@ -352,11 +360,12 @@
                     F[c, i, :, 1] = p1 + add[:, 1]
                     F[c, i, :, 2] = p2
                 F[c, i, :, 0] = p0 + jnp.where((half == 0) & (lane > 0), roll_l(p2, 1), 0.0)
-            for j in range(5):
-                x0, x4 = F[c, 0, j], F[c, 4, j]
-                F[c, 0, j] = x0 + jnp.where(bit_a == 1, roll_s(x4, 1), 0.0)
-                F[c, 4, j] = x4 + jnp.where(bit_a == 0, roll_s(x0, -1), 0.0)
-            for i in range(5):
+            if 0 in planes:
+                for j in range(5):
+                    x0, x4 = F[c, 0, j], F[c, 4, j]
+                    F[c, 0, j] = x0 + jnp.where(bit_a == 1, roll_s(x4, 1), 0.0)
+                    F[c, 4, j] = x4 + jnp.where(bit_a == 0, roll_s(x0, -1), 0.0)
+            for i in planes:
                 x0, x4 = F[c, i, 0], F[c, i, 4]
                 F[c, i, 0] = x0 + jnp.where(bit_b == 1, roll_s(x4, 2), 0.0)
                 F[c, i, 4] = x4 + jnp.where(bit_b == 0, roll_s(x0, -2), 0.0)
@@ -398,8 +407,9 @@
 
         return bit, width, value, at, line_at
 
-    def pack(comps, slot):
-        for side in (0, 1, 2, 3):
+    def pack(comps, slot, sides):
+        pack_corners(comps, slot, [side for side in sides if side >= 4])
+        for side in [side for side in sides if side < 4]:
             bit, width, value, at, line_at = face(side)
             tile = 0
             for g, group in enumerate(GROUPS[comps]):
@@ -420,7 +430,9 @@
                     send[side][slot, tile] = x.astype(jnp.int32).astype(jnp.int16)
                     tile += 1
             start(side, comps, slot)
-        for side in range(4, 8):
+
+    def pack_corners(comps, slot, sides):
+        for side in sides:
             da, db = SIDES[side]
             va, vb = (da + 1) // 2, (db + 1) // 2
             items = []
@@ -433,8 +445,8 @@
                 send[side][slot, n // 2 : n // 2 + 1] = merge(items[n], y, bit_b, 2, vb)
             start(side, comps, slot)
 
-    def unpack(comps, slot):
-        for side in (2, 3, 0, 1):
+    def unpack(comps, slot, sides):
+        for side in [side for side in sides if side < 4]:
             finish(side, comps, slot)
             bit, width, value, at, line_at = face(side)
             tile = 0
@@ -453,7 +465,7 @@
                 for m, c in enumerate(group):
                     for n in range(5):
                         F[at(c, n, 2)] = F[at(c, n, 2)] + end_of(last, 5 * m + n)[0]
-        for side in range(4, 8):
+        for side in [side for side in sides if side >= 4]:
             da, db = SIDES[side]
             va, vb = (da + 1) // 2, (db + 1) // 2
             items = []
@@ -530,10 +542,10 @@
             F[3, i, j] = CM[i, j] * quad(i, j)
             for c in range(3):
                 F[c, i, j] = U[c, i, j]
-    local_sums(4)
+    local_sums(4, (0, 4, 1, 2, 3))
     pl.semaphore_wait(barrier, devices - 1)
     send_rows()
-    pack(4, 0)
+    pack(4, 0, ENDS + SLABS)
     for one in loads[3:]:
         one.wait()
     load_pairs(LAM, raw_lame)
@@ -576,7 +588,7 @@
                         0:NODES6, first : first + 128
                     ]
 
-    unpack(4, 0)
+    unpack(4, 0, SLABS + ENDS)
     for i in range(5):
         for j in range(5):
             part = share(i, j)
@@ -592,19 +604,29 @@
     def stress(c, d):
         return pair[(min(c, d), max(c, d))]
 
+    def along_k(planes, js):
+        for c in range(3):
+            for i in planes:
+                for first, last in js:
+                    outs = kline(FORWARD, *(U[c, i, first:last, kp] for kp in range(3)), half)
+                    for kp in range(3):
+                        GR[2, c, i, first:last, kp] = outs[kp]
+
+    def along_j(planes):
+        for c in range(3):
+            for i in planes:
+                outs = line(FORWARD, [U[c, i, j] for j in range(5)])
+                for j in range(5):
+                    GR[1, c, i, j] = outs[j]
+
     def one_step(s, carry):
+        along_j((0, 4))
+        along_k((0, 4), ((0, 5),))
         for c in range(3):
             for j in range(5):
                 outs = line(FORWARD, [U[c, i, j] for i in range(5)])
                 for i in range(5):
                     GR[0, c, i, j] = outs[i]
-            for i in range(5):
-                outs = line(FORWARD, [U[c, i, j] for j in range(5)])
-                for j in range(5):
-                    GR[1, c, i, j] = outs[j]
-                outs = kline(FORWARD, U[c, i, :, 0], U[c, i, :, 1], U[c, i, :, 2], half)
-                for kp in range(3):
-                    GR[2, c, i, :, kp] = outs[kp]
         for i in range(5):
             for j in range(5):
                 g = [[GR[d, c, i, j] for c in range(3)] for d in range(3)]
@@ -615,20 +637,8 @@
                     SG[c, i, j] = mu2 * g[c][c] + vol
                     for d in range(c):
                         SG[stress(c, d), i, j] = mu * (g[c][d] + g[d][c])
-        for c in range(3):
-            for j in range(5):
-                outs = line(BACKWARD, [SG[stress(c, 0), i, j] for i in range(5)])
-                for i in range(5):
-                    F[c, i, j] = outs[i]
-            for i in range(5):
-                outs = line(BACKWARD, [SG[stress(c, 1), i, j] for j in range(5)])
-                for j in range(5):
-                    F[c, i, j] = F[c, i, j] + outs[j]
-                p = stress(c, 2)
-                outs = kline(BACKWARD, SG[p, i, :, 0], SG[p, i, :, 1], SG[p, i, :, 2], half)
-                for kp in range(3):
-                    F[c, i, :, kp] = F[c, i, :, kp] + outs[kp]
         slot = (s + 1) % 2
+        force((0, 4))
 
         @pl.when(s == 0)
         def _():
@@ -640,18 +650,44 @@
                     DEP[at : at + 120, :] = DEP[at : at + 120, :] + W[c, i].reshape(120, 128)
                     W[c, i] = jnp.zeros((5, 3, 8, 128), F32)
 
-        local_sums(3, DEP)
-        pack(3, slot)
+        local_sums(3, (0, 4), DEP)
+        pack(3, slot, ENDS)
+        force((1, 2, 3))
+        local_sums(3, (1, 2, 3), DEP)
+        pack(3, slot, SLABS)
 
         @pl.when(s < STEPS - 1)
         def _():
             deposit(s + 1)
 
-        inner = [(i, j) for i in range(1, 4) for j in range(1, 4)]
-        update(inner)
-        unpack(3, slot)
-        update([(i, j) for i in range(5) for j in range(5) if (i, j) not in inner])
+        update([(i, j) for i in range(1, 4) for j in range(1, 4)])
+        along_k((1, 2, 3), ((1, 4),))
+        unpack(3, slot, SLABS)
+        update([(i, j) for i in range(1, 4) for j in (0, 4)])
+
+        @pl.when(s < STEPS - 1)
+        def _():
+            along_k((1, 2, 3), ((0, 1), (4, 5)))
+            along_j((1, 2, 3))
+
+        unpack(3, slot, ENDS)
+        update([(i, j) for i in (0, 4) for j in range(5)])
         return carry
+
+    def force(planes):
+        for c in range(3):
+            for j in range(5):
+                outs = line(BACKWARD, [SG[stress(c, 0), i, j] for i in range(5)], planes)
+                for i in planes:
+                    F[c, i, j] = outs[i]
+            for i in planes:
+                outs = line(BACKWARD, [SG[stress(c, 1), i, j] for j in range(5)])
+                for j in range(5):
+                    F[c, i, j] = F[c, i, j] + outs[j]
+                p = stress(c, 2)
+                outs = kline(BACKWARD, SG[p, i, :, 0], SG[p, i, :, 1], SG[p, i, :, 2], half)
+                for kp in range(3):
+                    F[c, i, :, kp] = F[c, i, :, kp] + outs[kp]
 
     def update(lines):
         for i, j in lines:
@@ -661,6 +697,8 @@
                 W[c, i, j] = w
                 U[c, i, j] = U[c, i, j] + w
 
+    along_k((1, 2, 3), ((0, 5),))
+    along_j((1, 2, 3))
     lax.fori_loop(0, STEPS, one_step, 0)
     for i in range(5):
         for j in range(5):

time: 49.4 us -> 47.4 us (0.960); the launches traced: 49.3 us -> 46.7 us
  Pallas kernels: 47.2 us -> 44.6 us
    pallas_call x1, Pallas kernels: 47.2 us -> 44.6 us  [shards(): pl.pallas_call(functools.partial(step_kernel, nd, ns), out_shape=(out, ou...]
where the time goes in v4:
time: 47.4 us; the launch traced here: 46.7 us
  Pallas kernels  44.6 us (94%)
  other arithmetic  1.46 us (3%)
  between operations  0.64 us (1%)
    pallas_call x1, Pallas kernels, shards(): pl.pallas_call(functools.partial(step_kernel, nd, ns), out_shape=(out, ou...  44.6 us
    mul x1, other arithmetic, shards(): return (from_rows(disp + veloc), from_rows(veloc * (1.0 / DT)))  1.46 us

profile of v4, /device:TPU:6, one launch (start us, length us, event | category | flops | bytes accessed | tf_op | source)
XLA Modules:
  0.0 46.7 jit_solution(5968176080670847177)
XLA Ops:
  0.6 44.6 %time_steps.1 = (f32[3,5,5,5,4,128]{5,4,3,2,1,0:T(4,128)S(1)}, f32[3,5,5,5,4,128]{5,4,3,2,1,0:T(4,128)S(1)}) custom-call(f32[3,5,5,5,4,128]{5,4,3,2,1,0:T(4,128)} %bitcast.38, f32[3,5,5,5,4,128]{5,4,3,2,1,0:T(4,128)} %bitcast.39, f32[5,5,5,4,128]{4,3,2,1,0:T(4,128)} %bitcast.42, f32[5,5,5,4,128]{4,3,2,1,0:T(4,128)} %bitcast.43, ...), custom_call_target="tpu_custom_call" | custom-call | tf_op jit(solution)/shard_map/time_steps/pallas_call | solution.py:749
  45.3 1.5 %broadcast_multiply_fusion = (f32[3,5,5,5,4,128]{5,4,3,2,1,0:T(4,128)}, f32[3,5,5,5,4,128]{5,4,3,2,1,0:T(4,128)}) fusion(f32[3,5,5,5,4,128]{5,4,3,2,1,0:T(4,128)S(1)} %get-tuple-element.5, f32[3,5,5,5,4,128]{5,4,3,2,1,0:T(4,128)S(1)} %get-tuple-element.4), kind=kLoop, calls=%fused_computation | loop fusion | flops 384000 | bytes 3072000 | tf_op jit(solution)/shard_map/mul | solution.py:815

commit v5 on v4

--- a/solution.py
+++ b/solution.py
@@ -225,6 +225,7 @@
     DEP,
     TT,
     OH,
+    LEFT,
     *rest,
 ):
     send, recv = rest[0:8], rest[8:16]
@@ -343,12 +344,6 @@
             dst[lead + (kp, slice(0, 4))] = src[lead + (2 * kp,)]
             dst[lead + (kp, slice(4, 8))] = src[lead + (min(2 * kp + 1, 4),)]
 
-    def store_pairs(dst, src):
-        lead = (slice(None),) * (len(src.shape) - 3)
-        for k in range(5):
-            first = 4 * (k % 2)
-            dst[lead + (k,)] = src[lead + (k // 2, slice(first, first + 4))]
-
     def local_sums(comps, planes, extra=None):
         for c in range(comps):
             for i in planes:
@@ -408,7 +403,6 @@
         return bit, width, value, at, line_at
 
     def pack(comps, slot, sides):
-        pack_corners(comps, slot, [side for side in sides if side >= 4])
         for side in [side for side in sides if side < 4]:
             bit, width, value, at, line_at = face(side)
             tile = 0
@@ -421,8 +415,10 @@
                 largest = jnp.abs(rows[0])
                 for row in rows[1:]:
                     largest = jnp.maximum(largest, jnp.abs(row))
+                for shift in (4, 2, 1):
+                    largest = jnp.maximum(largest, roll_s(largest, shift))
                 scale = largest * (1.0 / 32000.0) + 1e-30
-                send_scale[side][slot, g : g + 1] = scale
+                send_scale[side][slot, g : g + 1] = scale[:, 0:1]
                 inverse = 1.0 / scale
                 for n in range(0, len(rows), 2):
                     x = jnp.concatenate([rows[n][0] * inverse[0], rows[n + 1][0] * inverse[0]], 0)
@@ -430,6 +426,7 @@
                     send[side][slot, tile] = x.astype(jnp.int32).astype(jnp.int16)
                     tile += 1
             start(side, comps, slot)
+        pack_corners(comps, slot, [side for side in sides if side >= 4])
 
     def pack_corners(comps, slot, sides):
         for side in sides:
@@ -451,7 +448,7 @@
             bit, width, value, at, line_at = face(side)
             tile = 0
             for g, group in enumerate(GROUPS[comps]):
-                scale = recv_scale[side][slot, g : g + 1]
+                scale = jnp.broadcast_to(recv_scale[side][slot, g : g + 1], (1, 8, 128))
                 rows = []
                 for _ in range(tiles_of(group)):
                     x = recv[side][slot, tile].astype(jnp.int32).astype(F32)
@@ -575,22 +572,23 @@
         for c in range(3):
             row = c * STEPS + s
             src = TT[pl.ds(HI + row, 1), :] + TT[pl.ds(LO + row, 1), :]
-            term = TT[0:152, :] * src
+            term = TT[0:160, :] * src
             high = term.astype(BF16)
-            low = (term - high.astype(F32)).astype(BF16)
-            sums = jnp.dot(high, OH[...], preferred_element_type=F32) + jnp.dot(
-                low, OH[...], preferred_element_type=F32
-            )
+            LEFT[c * 320 : c * 320 + 160, :] = high
+            LEFT[c * 320 + 160 : c * 320 + 320, :] = (term - high.astype(F32)).astype(BF16)
+        sums = jnp.dot(LEFT[...], OH[...], preferred_element_type=F32)
+        for c in range(3):
+            first = c * 320
+            both = sums[first : first + 152, :] + sums[first + 160 : first + 312, :]
             for a in range(2):
                 for b in range(2):
-                    q, first = b * 2 + a, (a * 2 + b) * 128
-                    DEP[pl.ds(c * 600 + q, NODES6, stride=4), :] = sums[
-                        0:NODES6, first : first + 128
+                    q, col = b * 2 + a, (a * 2 + b) * 128
+                    DEP[pl.ds(c * 600 + q, NODES6, stride=4), :] = both[
+                        0:NODES6, col : col + 128
                     ]
 
-    unpack(4, 0, SLABS + ENDS)
-    for i in range(5):
-        for j in range(5):
+    def begin(lines):
+        for i, j in lines:
             part = share(i, j)
             mass = close_k(F[3, i, j])
             CM[i, j] = (DT * DT) / mass
@@ -598,6 +596,10 @@
             for c in range(3):
                 U[c, i, j] = close_k(F[c, i, j]) * part
                 W[c, i, j] = W[c, i, j] * scaled
+
+    inner = [(i, j) for i in range(1, 4) for j in range(1, 4)]
+    rims = [(i, j) for i in range(1, 4) for j in (0, 4)]
+    outer = [(i, j) for i in (0, 4) for j in range(5)]
 
     pair = {(0, 0): 0, (1, 1): 1, (2, 2): 2, (0, 1): 3, (0, 2): 4, (1, 2): 5}
 
@@ -653,6 +655,7 @@
         local_sums(3, (0, 4), DEP)
         pack(3, slot, ENDS)
         force((1, 2, 3))
+
         local_sums(3, (1, 2, 3), DEP)
         pack(3, slot, SLABS)
 
@@ -660,10 +663,10 @@
         def _():
             deposit(s + 1)
 
-        update([(i, j) for i in range(1, 4) for j in range(1, 4)])
+        update(inner)
         along_k((1, 2, 3), ((1, 4),))
         unpack(3, slot, SLABS)
-        update([(i, j) for i in range(1, 4) for j in (0, 4)])
+        update(rims)
 
         @pl.when(s < STEPS - 1)
         def _():
@@ -671,8 +674,17 @@
             along_j((1, 2, 3))
 
         unpack(3, slot, ENDS)
-        update([(i, j) for i in (0, 4) for j in range(5)])
+        update(outer)
         return carry
+
+    def leave(planes):
+        for c in range(3):
+            for i in planes:
+                U[c, i] = U[c, i] - W[c, i]
+                for k in range(5):
+                    rows = slice(4 * (k % 2), 4 * (k % 2) + 4)
+                    disp_out[c, i, :, k] = U[c, i, :, k // 2, rows]
+                    veloc_out[c, i, :, k] = W[c, i, :, k // 2, rows]
 
     def force(planes):
         for c in range(3):
@@ -697,15 +709,16 @@
                 W[c, i, j] = w
                 U[c, i, j] = U[c, i, j] + w
 
-    along_k((1, 2, 3), ((0, 5),))
+    begin(inner)
+    along_k((1, 2, 3), ((1, 4),))
+    unpack(4, 0, SLABS)
+    begin(rims)
+    along_k((1, 2, 3), ((0, 1), (4, 5)))
     along_j((1, 2, 3))
+    unpack(4, 0, ENDS)
+    begin(outer)
     lax.fori_loop(0, STEPS, one_step, 0)
-    for i in range(5):
-        for j in range(5):
-            for c in range(3):
-                U[c, i, j] = U[c, i, j] - W[c, i, j]
-    store_pairs(disp_out, U)
-    store_pairs(veloc_out, W)
+    leave((0, 1, 2, 3, 4))
 
 
 def to_rows(x):
@@ -744,7 +757,7 @@
     tiles, scales, ends = sizes(4)
     messages = [pltpu.VMEM((2, tiles, 16, 128), jnp.int16) for side in range(4)]
     messages += [vm(2, ends, 8, 128) for side in range(4)]
-    factors = [vm(2, scales, 8, 128) for side in range(4)]
+    factors = [vm(2, scales, 1, 128) for side in range(4)]
     out = jax.ShapeDtypeStruct((3, 5, 5, 5, 4, EC), F32)
     disp, veloc = pl.pallas_call(
         functools.partial(step_kernel, nd, ns),
@@ -780,6 +793,7 @@
             vm(1808, 128),
             vm(256, CAP * devices),
             pltpu.VMEM((CAP * devices, 512), BF16),
+            pltpu.VMEM((960, CAP * devices), BF16),
             *messages,
             *messages,
             *factors,

time: 47.4 us -> 46.9 us (0.989)
  Pallas kernels: 44.6 us -> 44 us
    pallas_call x1, Pallas kernels: 44.6 us -> 44 us  [shards(): pl.pallas_call(functools.partial(step_kernel, nd, ns), out_shape=(out, ou...]
where the time goes in v5:
time: 46.9 us; the launch traced here: 46.1 us
  Pallas kernels  44 us (94%)
  other arithmetic  1.46 us (3%)
  between operations  0.64 us (1%)
    pallas_call x1, Pallas kernels, shards(): pl.pallas_call(functools.partial(step_kernel, nd, ns), out_shape=(out, ou...  44 us
    mul x1, other arithmetic, shards(): return (from_rows(disp + veloc), from_rows(veloc * (1.0 / DT)))  1.46 us

profile of v5, /device:TPU:6, one launch (start us, length us, event | category | flops | bytes accessed | tf_op | source)
XLA Modules:
  0.0 46.1 jit_solution(4122520556204285335)
XLA Ops:
  0.6 44.0 %time_steps.1 = (f32[3,5,5,5,4,128]{5,4,3,2,1,0:T(4,128)S(1)}, f32[3,5,5,5,4,128]{5,4,3,2,1,0:T(4,128)S(1)}) custom-call(f32[3,5,5,5,4,128]{5,4,3,2,1,0:T(4,128)} %bitcast.38, f32[3,5,5,5,4,128]{5,4,3,2,1,0:T(4,128)} %bitcast.39, f32[5,5,5,4,128]{4,3,2,1,0:T(4,128)} %bitcast.42, f32[5,5,5,4,128]{4,3,2,1,0:T(4,128)} %bitcast.43, ...), custom_call_target="tpu_custom_call" | custom-call | tf_op jit(solution)/shard_map/time_steps/pallas_call | solution.py:762
  44.7 1.5 %broadcast_multiply_fusion = (f32[3,5,5,5,4,128]{5,4,3,2,1,0:T(4,128)}, f32[3,5,5,5,4,128]{5,4,3,2,1,0:T(4,128)}) fusion(f32[3,5,5,5,4,128]{5,4,3,2,1,0:T(4,128)S(1)} %get-tuple-element.5, f32[3,5,5,5,4,128]{5,4,3,2,1,0:T(4,128)S(1)} %get-tuple-element.4), kind=kLoop, calls=%fused_computation | loop fusion | flops 384000 | bytes 3072000 | tf_op jit(solution)/shard_map/mul | solution.py:829

commit v6 on v5

--- a/solution.py
+++ b/solution.py
@@ -415,10 +415,8 @@
                 largest = jnp.abs(rows[0])
                 for row in rows[1:]:
                     largest = jnp.maximum(largest, jnp.abs(row))
-                for shift in (4, 2, 1):
-                    largest = jnp.maximum(largest, roll_s(largest, shift))
                 scale = largest * (1.0 / 32000.0) + 1e-30
-                send_scale[side][slot, g : g + 1] = scale[:, 0:1]
+                send_scale[side][slot, g : g + 1] = scale
                 inverse = 1.0 / scale
                 for n in range(0, len(rows), 2):
                     x = jnp.concatenate([rows[n][0] * inverse[0], rows[n + 1][0] * inverse[0]], 0)
@@ -448,7 +446,7 @@
             bit, width, value, at, line_at = face(side)
             tile = 0
             for g, group in enumerate(GROUPS[comps]):
-                scale = jnp.broadcast_to(recv_scale[side][slot, g : g + 1], (1, 8, 128))
+                scale = recv_scale[side][slot, g : g + 1]
                 rows = []
                 for _ in range(tiles_of(group)):
                     x = recv[side][slot, tile].astype(jnp.int32).astype(F32)
@@ -757,7 +755,7 @@
     tiles, scales, ends = sizes(4)
     messages = [pltpu.VMEM((2, tiles, 16, 128), jnp.int16) for side in range(4)]
     messages += [vm(2, ends, 8, 128) for side in range(4)]
-    factors = [vm(2, scales, 1, 128) for side in range(4)]
+    factors = [vm(2, scales, 8, 128) for side in range(4)]
     out = jax.ShapeDtypeStruct((3, 5, 5, 5, 4, EC), F32)
     disp, veloc = pl.pallas_call(
         functools.partial(step_kernel, nd, ns),

time: 46.9 us -> 47 us (level)
  no operation moved by 1% of the time
where the time goes in v6:
time: 47 us; the launch traced here: 46.5 us
  Pallas kernels  44.4 us (94%)
  other arithmetic  1.46 us (3%)
  between operations  0.64 us (1%)
    pallas_call x1, Pallas kernels, shards(): pl.pallas_call(functools.partial(step_kernel, nd, ns), out_shape=(out, ou...  44.4 us
    mul x1, other arithmetic, shards(): return (from_rows(disp + veloc), from_rows(veloc * (1.0 / DT)))  1.46 us

profile of v6, /device:TPU:6, one launch (start us, length us, event | category | flops | bytes accessed | tf_op | source)
XLA Modules:
  0.0 46.5 jit_solution(1876346104398961575)
XLA Ops:
  0.6 44.4 %time_steps.1 = (f32[3,5,5,5,4,128]{5,4,3,2,1,0:T(4,128)S(1)}, f32[3,5,5,5,4,128]{5,4,3,2,1,0:T(4,128)S(1)}) custom-call(f32[3,5,5,5,4,128]{5,4,3,2,1,0:T(4,128)} %bitcast.38, f32[3,5,5,5,4,128]{5,4,3,2,1,0:T(4,128)} %bitcast.39, f32[5,5,5,4,128]{4,3,2,1,0:T(4,128)} %bitcast.42, f32[5,5,5,4,128]{4,3,2,1,0:T(4,128)} %bitcast.43, ...), custom_call_target="tpu_custom_call" | custom-call | tf_op jit(solution)/shard_map/time_steps/pallas_call | solution.py:760
  45.0 1.5 %broadcast_multiply_fusion = (f32[3,5,5,5,4,128]{5,4,3,2,1,0:T(4,128)}, f32[3,5,5,5,4,128]{5,4,3,2,1,0:T(4,128)}) fusion(f32[3,5,5,5,4,128]{5,4,3,2,1,0:T(4,128)S(1)} %get-tuple-element.5, f32[3,5,5,5,4,128]{5,4,3,2,1,0:T(4,128)S(1)} %get-tuple-element.4), kind=kLoop, calls=%fused_computation | loop fusion | flops 384000 | bytes 3072000 | tf_op jit(solution)/shard_map/mul | solution.py:827
